TPU v7x, 128 devices: a whole 4x4x4 slice. The times are simulated.
128 devices in a mesh: freq: 16 (over x, y), slab: 8 (over z, core).
Axes of the slice: x: 4, y: 4, z: 4, core: 2. Of those that a mesh axis runs over, the one named last changes fastest.
Arguments:
- fine_model: bfloat16 [2048, 2048], P(('freq', 'slab')), may hold values from 0.5 to 2
- resample: bfloat16 [16, 1024, 2048], P('freq', 'slab'), may hold values from -0.125 to 0.125
- lateral: bfloat16 [2048, 2048], replicated, may hold values from -0.0625 to 0.0625
- shift: float32 [16], P('freq'), may hold values from 0.5 to 4
- source: float32 [16, 1024, 2048], P('freq', 'slab'), may hold values from -6 to 6
- receiver: float32 [16, 1024, 2048], P('freq', 'slab'), may hold values from -6 to 6
Outputs:
- image: float32 [2048, 2048], P(('freq', 'slab'))
All inputs are finite; a program needn't handle non-finite values.
Results may differ from a plain program's by a relative error of at most 0.0029.
Values may be sent and summed in bfloat16 or wider, within the bound.
A program may use at most 128 MiB of HBM per device.

v0:
```python
import jax
import jax.numpy as jnp
from jax import lax
from jax.sharding import PartitionSpec as P

SWEEPS = 8


def with_halo(value, sides, width):
    for axis, dim in sides:
        size, length = (lax.axis_size(axis), value.shape[dim])
        up = [(i, (i + 1) % size) for i in range(size - 1)]
        down = [(j, i) for i, j in up]
        last = lax.slice_in_dim(value, length - width, length, axis=dim)
        initial = lax.slice_in_dim(value, 0, width, axis=dim)
        before = lax.ppermute(last, axis, up)
        after = lax.ppermute(initial, axis, down)
        value = jnp.concatenate([before, value, after], axis=dim)
    return value


def shards(fine_model, resample, lateral, shift, source, receiver):
    oper = resample[0]
    columns = oper
    coarse = jnp.dot(
        columns,
        lax.all_gather(fine_model, ("freq", "slab"), axis=0, tiled=True),
        preferred_element_type=jnp.float32,
    )
    diag = 4.0 + shift[0] * coarse * coarse
    src = source[0]
    field = jnp.zeros(src.shape, jnp.float32)
    for sweep in range(SWEEPS):
        padded = with_halo(field, (("slab", 0),), 1)
        beside = padded[2:] + padded[:-2]
        side = jnp.dot(field.astype(jnp.bfloat16), lateral, preferred_element_type=jnp.float32)
        field = (src + 0.5 * beside + side) / diag
    partial_img = (field * receiver[0]).astype(jnp.bfloat16)
    columns = oper
    return lax.psum_scatter(
        lax.dot_general(
            columns, partial_img, (((0,), (0,)), ((), ())), preferred_element_type=jnp.float32
        ),
        ("freq", "slab"),
        scatter_dimension=0,
        tiled=True,
    )


def solution(mesh):
    in_specs = (
        P(("freq", "slab"), None),
        P("freq", "slab", None),
        P(),
        P("freq"),
        P("freq", "slab", None),
        P("freq", "slab", None),
    )
    out_specs = P(("freq", "slab"), None)
    return jax.shard_map(shards, mesh=mesh, in_specs=in_specs, out_specs=out_specs, check_vma=False)
```

profile of v0, /device:TPU:1, one launch (start us, length us, event | category | flops | bytes accessed | tf_op | source)
XLA Modules:
  0.0 842.6 jit_solution(14113085635344979376)
XLA Ops:
  7.3 4.9 collective-permute-start.1
  12.3 1.9 collective-permute-start
  14.8 69.3 %all-gather.2.cloned.1.call-done = bf16[2048,2048]{1,0:T(8,128)(2,1)} async-done(((bf16[16,2048]{1,0:T(8,128)(2,1)}), bf16[2048,2048]{1,0:T(8,128)(2,1)}) %all-gather.2.cloned.1.call-update) | async-done | bytes 8388624 | tf_op jit(solution)/shard_map/all_gather | solution.py:27
  84.1 4.8 fusion.5
  91.3 2.2 collective-permute-start.2
  93.5 3.4 collective-permute-start.3
  97.7 1.6 fusion.41
  99.3 1.9 collective-permute-start.4
  101.3 4.2 collective-permute-start.5
  107.9 1.9 collective-permute-start.6
  109.8 4.2 collective-permute-start.7
  116.4 1.9 collective-permute-start.8
  118.3 4.2 collective-permute-start.9
  123.3 1.6 fusion.26
  124.9 1.9 collective-permute-start.10
  126.9 4.3 collective-permute-start.11
  132.0 1.6 fusion.21
  133.6 1.9 collective-permute-start.12
  135.5 4.4 collective-permute-start.13
  142.1 1.9 collective-permute-start.14
  144.0 4.2 collective-permute-start.15
  149.0 12.7 %convolution_bitcast_fusion = f32[2048,2048]{0,1:T(8,128)} fusion(f32[1,128,2048]{2,1,0:T(8,128)} %param.11, f32[128,2048]{1,0:T(8,128)S(1)} %fusion.5, f32[128,2048]{1,0:T(8,128)S(1)} %fusion.16, f32[1,2048]{1,0:T(1,128)S(1)} %collective-permute-done.15, f32[1,2048]{1,0:T(1,128)S(1)} %collective-permute-done.14, f32[1,128,2048]{2,1,0:T(8,128)} %param.10, ...), kind=kOutput, calls=%fused_computation | convolution fusion | flops 2150105088 | bytes 29900800 | tf_op jit(solution)/shard_map/dot_general | solution.py:41
  161.7 17.6 %copy.9 = f32[2048,2048]{1,0:T(8,128)} copy(f32[2048,2048]{0,1:T(8,128)} %convolution_bitcast_fusion) | data formatting | bytes 33554432
  179.3 656.4 %reduce-scatter.4.cloned.1.call-done = f32[16,2048]{1,0:T(8,128)} async-done(((f32[2048,2048]{1,0:T(8,128)}), f32[16,2048]{1,0:T(8,128)}) %reduce-scatter.4.cloned.1.call-update) | async-done | bytes 131088 | tf_op jit(solution)/shard_map/reduce_scatter | solution.py:40
  (43 shorter events, 13.2 us)
Async XLA Ops:
  6.5 77.6 %copy-start = (bf16[1,128,2048]{2,1,0:T(8,128)(2,1)S(1)}, bf16[1,128,2048]{2,1,0:T(8,128)(2,1)}, u32[]{:S(2)}) copy-start(bf16[1,128,2048]{2,1,0:T(8,128)(2,1)} %param.7) | copy-start | bytes 1572868
  6.5 82.4 %copy-start.1 = (f32[1,128,2048]{2,1,0:T(8,128)S(1)}, f32[1,128,2048]{2,1,0:T(8,128)}, u32[]{:S(2)}) copy-start(f32[1,128,2048]{2,1,0:T(8,128)} %param.10) | copy-start | bytes 3145732
  6.5 77.6 %all-gather.2.cloned.1.call-start = ((), (), s32[]{:S(2)}) async-start(), calls=%async_computation.1 | async-start | bytes 8454144 | tf_op jit(solution)/shard_map/all_gather | solution.py:27
  7.3 828.5 %reduce-scatter.4.cloned.1.call-start = ((), (), s32[]{:S(2)}) async-start(), calls=%async_computation.2 | async-start | bytes 16908288 | tf_op jit(solution)/shard_map/reduce_scatter | solution.py:40
  7.3 81.6 %collective-permute-start.1 = (f32[1,2048]{1,0:T(1,128)S(1)}, f32[1,2048]{1,0:T(1,128)S(1)}, u32[]{:S(2)}, u32[]{:S(2)}) collective-permute-start(f32[1,2048]{1,0:T(1,128)S(1)} %broadcast.12), channel_id=1, source_target_pairs={{0,1},{1,2},{2,3},{3,4},{4,5},{5,6},{6,7},{8,9},{9,10},{10,11},{11... | collective-permute-start | bytes 24584 | tf_op jit(solution)/shard_map/ppermute | solution.py:16
  12.3 76.7 %collective-permute-start = (f32[1,2048]{1,0:T(1,128)S(1)}, f32[1,2048]{1,0:T(1,128)S(1)}, u32[]{:S(2)}, u32[]{:S(2)}) collective-permute-start(f32[1,2048]{1,0:T(1,128)S(1)} %broadcast.12), channel_id=1, source_target_pairs={{1,0},{2,1},{3,2},{4,3},{5,4},{6,5},{7,6},{9,8},{10,9},{11,10},{12... | collective-permute-start | bytes 24584 | tf_op jit(solution)/shard_map/ppermute | solution.py:17
  84.1 4.8 slice-start
  84.1 5.8 slice-start.1
  91.3 5.6 collective-permute-start.2
  93.5 4.2 collective-permute-start.3
  99.3 6.1 collective-permute-start.4
  101.3 5.0 collective-permute-start.5
  107.9 6.1 collective-permute-start.6
  109.8 5.0 collective-permute-start.7
  116.4 6.1 collective-permute-start.8
  118.3 5.0 collective-permute-start.9
  124.9 6.3 collective-permute-start.10
  126.8 13.6 %copy-start.2 = (f32[1,128,2048]{2,1,0:T(8,128)S(1)}, f32[1,128,2048]{2,1,0:T(8,128)}, u32[]{:S(2)}) copy-start(f32[1,128,2048]{2,1,0:T(8,128)} %param.10) | copy-start | bytes 3145732
  126.9 5.1 collective-permute-start.11
  133.6 6.3 collective-permute-start.12
  135.5 5.0 collective-permute-start.13
  142.1 6.1 collective-permute-start.14
  144.0 5.0 collective-permute-start.15
Sparse Core Ops, SparseCore 0:
  10.3 73.7 all-gather.1
  179.4 656.2 reduce-scatter.3
where the time goes:
time: 850 us; the launch traced here: 843 us
  waiting for transfers between devices  732 us (86%)
  starting transfers between devices  49.4 us (6%)
  matrix products  28.4 us (3%)
  local copies, waits for them, and re-layouts  18.7 us (2%)
  between operations  14.4 us (2%)
    reduce_scatter x1, waiting for transfers between devices, shards(): lax.psum_scatter(lax.dot_general(columns, partial_img, (((0,), (0,)), (()...  656 us
    all_gather x1, waiting for transfers between devices, shards(): lax.all_gather(fine_model, ('freq', 'slab'), axis=0, tiled=True)  69.3 us
    ppermute x8, starting transfers between devices, with_halo(): before = lax.ppermute(last, axis, up)  33.8 us
    unnamed x11, local copies, waits for them, and re-layouts  18.6 us
  transfers between devices with their start and end apart: 18, of which 9 were waited for; matrix products, arithmetic and copies ran while one was open for 1% of the time, Pallas kernels for 0%

commit v1 on v0

v1 whole, which is shorter than its diff:
```python
import jax
import jax.numpy as jnp
from jax import lax
from jax.sharding import PartitionSpec as P

SWEEPS = 8
HALO = 8


def with_halo(value, size):
    up = [(i, i + 1) for i in range(size - 1)]
    down = [(i + 1, i) for i in range(size - 1)]
    before = lax.ppermute(value[-HALO:], "slab", up)
    after = lax.ppermute(value[:HALO], "slab", down)
    return jnp.concatenate([before, value, after], axis=0)


def shards(fine_model, resample, lateral, shift, source, receiver):
    freqs, slabs = lax.axis_size("freq"), lax.axis_size("slab")
    oper = resample[0]
    rows = oper.shape[0]
    every = lax.all_gather(oper, "slab", axis=0, tiled=True)
    wide = with_halo(oper, slabs)
    src = with_halo(source[0], slabs)
    model = lax.all_gather(fine_model, ("freq", "slab"), axis=0, tiled=True)
    coarse = jnp.dot(wide, model, preferred_element_type=jnp.float32)
    at = lax.axis_index("slab") * rows - HALO + lax.broadcasted_iota(jnp.int32, (rows + 2 * HALO, 1), 0)
    inside = (at >= 0) & (at < rows * slabs)
    inv = jnp.where(inside, 1.0 / (4.0 + shift[0] * coarse * coarse), 0.0)
    field = src * inv
    for sweep in range(1, SWEEPS):
        padded = jnp.pad(field, ((1, 1), (0, 0)))
        beside = padded[2:] + padded[:-2]
        side = jnp.dot(field.astype(jnp.bfloat16), lateral, preferred_element_type=jnp.float32)
        field = (src + 0.5 * beside + side) * inv
    part = (field[HALO:-HALO] * receiver[0]).astype(jnp.bfloat16)
    cols = lax.all_to_all(part, "slab", split_axis=1, concat_axis=0, tiled=True)
    term = lax.dot_general(every, cols, (((0,), (0,)), ((), ())), preferred_element_type=jnp.float32)
    mine = lax.psum_scatter(term, "freq", scatter_dimension=0, tiled=True)
    return lax.all_to_all(mine, "slab", split_axis=0, concat_axis=1, tiled=True)


def solution(mesh):
    in_specs = (
        P(("freq", "slab"), None),
        P("freq", "slab", None),
        P(),
        P("freq"),
        P("freq", "slab", None),
        P("freq", "slab", None),
    )
    out_specs = P(("freq", "slab"), None)
    return jax.shard_map(shards, mesh=mesh, in_specs=in_specs, out_specs=out_specs, check_vma=False)
```

time: 850 us -> 219 us (0.26)
  waiting for transfers between devices: 732 us -> 149 us
  starting transfers between devices: 49.4 us -> 16.1 us
  local copies, waits for them, and re-layouts: 18.7 us -> 5.6 us
  blocking collectives: 0 us -> 11.9 us
    reduce_scatter x1, waiting for transfers between devices: 656 us -> 73.9 us  [shards(): mine = lax.psum_scatter(term, 'freq', scatter_dimension=0, tiled=True)]
    ppermute x16 -> x4, starting transfers between devices: 49.4 us -> 12.4 us  [the longest x2 8.57 us: with_halo(): before = lax.ppermute(value[-HALO:], 'slab', up)]
    unnamed x11 -> x8, local copies, waits for them, and re-layouts: 18.6 us -> 1.05 us
    all_to_all x0 -> x1, blocking collectives: none -> 11.9 us  [shards(): return lax.all_to_all(mine, 'slab', split_axis=0, concat_axis=1, tiled=True)]
    all_gather x1 -> x2, waiting for transfers between devices: 69.3 us -> 71.6 us  [the longest x1 59.4 us: shards(): model = lax.all_gather(fine_model, ('freq', 'slab'), axis=0, tiled=True)]
  transfers between devices with their start and end apart: 18 -> 8, of which waited for: 9 -> 5; matrix products, arithmetic and copies ran while one was open for 1% -> 9% of each run, Pallas kernels for 0% -> 0%
where the time goes in v1:
time: 219 us; the launch traced here: 218 us
  waiting for transfers between devices  149 us (68%)
  matrix products  21.2 us (10%)
  starting transfers between devices  16.1 us (7%)
  between operations  13.9 us (6%)
  blocking collectives  11.9 us (5%)
  local copies, waits for them, and re-layouts  5.6 us (3%)
    reduce_scatter x1, waiting for transfers between devices, shards(): mine = lax.psum_scatter(term, 'freq', scatter_dimension=0, tiled=True)  73.9 us
    all_gather x1, waiting for transfers between devices, shards(): model = lax.all_gather(fine_model, ('freq', 'slab'), axis=0, tiled=True)  59.4 us
    all_gather x1, waiting for transfers between devices, shards(): every = lax.all_gather(oper, 'slab', axis=0, tiled=True)  12.3 us
    all_to_all x1, blocking collectives, shards(): return lax.all_to_all(mine, 'slab', split_axis=0, concat_axis=1, tiled=True)  11.9 us
    dot_general x7, matrix products, shards(): jnp.dot(field.astype(jnp.bfloat16), lateral, preferred_element_type=jnp.f...  10.9 us
    ppermute x2, starting transfers between devices, with_halo(): before = lax.ppermute(value[-HALO:], 'slab', up)  8.57 us
    dot_general x1, matrix products, shards(): coarse = jnp.dot(wide, model, preferred_element_type=jnp.float32)  5.46 us
    dot_general x1, matrix products, shards(): lax.dot_general(every, cols, (((0,), (0,)), ((), ())), preferred_element_...  4.78 us
  transfers between devices with their start and end apart: 8, of which 5 were waited for; matrix products, arithmetic and copies ran while one was open for 9% of the time, Pallas kernels for 0%

profile of v1, /device:TPU:1, one launch (start us, length us, event | category | flops | bytes accessed | tf_op | source)
XLA Modules:
  0.0 218.3 jit_solution(8704276760987448156)
XLA Ops:
  7.3 0.9 slice_bitcast_fusion.1
  8.2 4.9 %collective-permute-start = (f32[8,2048]{1,0:T(8,128)S(1)}, f32[8,2048]{1,0:T(8,128)S(1)}, u32[]{:S(2)}, u32[]{:S(2)}) collective-permute-start(f32[8,2048]{1,0:T(8,128)S(1)} %get-tuple-element.9), channel_id=1, source_target_pairs={{0,1},{1,2},{2,3},{3,4},{4,5},{5,6},{6,7},{8,9},{9,10},{10,11},{11... | collective-permute-start | bytes 196616 | tf_op jit(solution)/shard_map/ppermute | solution.py:13
  13.1 1.9 collective-permute-start.1
  15.1 0.8 slice_bitcast_fusion.3
  15.9 3.6 %collective-permute-start.2 = (bf16[8,2048]{1,0:T(8,128)(2,1)S(1)}, bf16[8,2048]{1,0:T(8,128)(2,1)S(1)}, u32[]{:S(2)}, u32[]{:S(2)}) collective-permute-start(bf16[8,2048]{1,0:T(8,128)(2,1)S(1)} %get-tuple-element.11), channel_id=1, source_target_pairs={{0,1},{1,2},{2,3},{3,4},{4,5},{5,6},{6,7},{8,9},{9,10},{10,11},{11... | collective-permute-start | bytes 98312 | tf_op jit(solution)/shard_map/ppermute | solution.py:13
  19.5 1.9 collective-permute-start.3
  22.1 2.6 %collective-permute-done.3 = bf16[8,2048]{1,0:T(8,128)(2,1)S(1)} collective-permute-done((bf16[8,2048]{1,0:T(8,128)(2,1)S(1)}, bf16[8,2048]{1,0:T(8,128)(2,1)S(1)}, u32[]{:S(2)}, u32[]{:S(2)}) %collective-permute-start.3) | collective-permute-done | bytes 32800 | tf_op jit(solution)/shard_map/ppermute | solution.py:14
  24.7 59.4 %all-gather.4.cloned.1.call-done = bf16[2048,2048]{1,0:T(8,128)(2,1)} async-done(((bf16[16,2048]{1,0:T(8,128)(2,1)}), bf16[2048,2048]{1,0:T(8,128)(2,1)}) %all-gather.4.cloned.1.call-update) | async-done | bytes 8388624 | tf_op jit(solution)/shard_map/all_gather | solution.py:25
  84.1 5.5 %pad_maximum_fusion = (f32[144,2048]{1,0:T(8,128)S(1)}, f32[144,2048]{1,0:T(8,128)S(1)}, f32[144,2048]{1,0:T(8,128)S(1)}) fusion(f32[8,2048]{1,0:T(8,128)S(1)} %collective-permute-done.1, f32[128,2048]{1,0:T(8,128)} %bitcast.43, f32[8,2048]{1,0:T(8,128)S(1)} %collective-permute-done, bf16[2048,2048]{1,0:T(8,128)(2,1)} %all-gather.4.cloned.1.call-done, ...), kind=kOutput, calls=%fused_computation.51 | convolution fusion | flops 1212088320 | bytes 13697172 | tf_op jit(solution)/shard_map/dot_general | solution.py:26
  89.6 0.8 slice-done.1
  90.7 1.6 fusion.9
  92.3 1.6 fusion.14
  93.9 1.6 fusion.19
  95.5 1.6 fusion.24
  97.1 1.6 fusion.29
  98.7 1.6 fusion.34
  100.7 1.4 fusion.49
  102.7 0.8 copy.16
  103.5 3.7 %all-to-all-start = ((bf16[128,8,256]{2,0,1:T(8,128)(2,1)}), bf16[128,8,256]{2,0,1:T(8,128)(2,1)S(1)}, u32[]{:S(2)}, u32[]{:S(2)}) async-start(bf16[128,8,256]{2,0,1:T(8,128)(2,1)} %bitcast.39), calls=%async_computation | async-start | bytes 1048576 | tf_op jit(solution)/shard_map/all_to_all | solution.py:37
  107.2 12.3 %all-gather.6.cloned.1.call-done = bf16[1,1024,2048]{2,1,0:T(8,128)(2,1)} async-done(((bf16[1,128,2048]{2,1,0:T(8,128)(2,1)}), bf16[1,1024,2048]{2,1,0:T(8,128)(2,1)}) %all-gather.6.cloned.1.call-update) | async-done | bytes 4194320 | tf_op jit(solution)/shard_map/all_gather | solution.py:22
  119.6 4.8 %fusion.2 = f32[2048,256]{0,1:T(8,128)} fusion(bf16[1024,256]{1,0:T(8,128)(2,1)S(1)} %bitcast.52, bf16[1,1024,2048]{2,1,0:T(8,128)(2,1)} %all-gather.6.cloned.1.call-done), kind=kOutput, calls=%fused_computation.2 | convolution fusion | flops 1073741824 | bytes 6815744 | tf_op jit(solution)/shard_map/dot_general | solution.py:38
  124.4 73.9 %reduce-scatter.2.cloned.1.call-done = f32[128,256]{0,1:T(8,128)} async-done(((f32[2048,256]{0,1:T(8,128)}), f32[128,256]{0,1:T(8,128)}) %reduce-scatter.2.cloned.1.call-update) | async-done | bytes 131088 | tf_op jit(solution)/shard_map/reduce_scatter | solution.py:39
  198.3 1.0 copy.11
  199.3 11.9 %all_to_all.38 = f32[8,16,256]{2,1,0:T(8,128)S(1)} all-to-all(f32[8,16,256]{2,1,0:T(8,128)S(1)} %bitcast.53), channel_id=1, replica_groups=mesh['freq'=16,'slab'=8] {'slab'}, dimensions={0} | all-to-all | bytes 262144 | tf_op jit(solution)/shard_map/all_to_all | solution.py:40
  (22 shorter events, 2.8 us)
Async XLA Ops:
  6.5 77.6 %all-gather.4.cloned.1.call-start = ((), (), s32[]{:S(2)}) async-start(), calls=%async_computation.3 | async-start | bytes 8454144 | tf_op jit(solution)/shard_map/all_gather | solution.py:25
  7.3 112.2 %all-gather.6.cloned.1.call-start = ((), (), s32[]{:S(2)}) async-start(), calls=%async_computation.5 | async-start | bytes 4718592 | tf_op jit(solution)/shard_map/all_gather | solution.py:22
  8.2 16.6 %collective-permute-start = (f32[8,2048]{1,0:T(8,128)S(1)}, f32[8,2048]{1,0:T(8,128)S(1)}, u32[]{:S(2)}, u32[]{:S(2)}) collective-permute-start(f32[8,2048]{1,0:T(8,128)S(1)} %get-tuple-element.9), channel_id=1, source_target_pairs={{0,1},{1,2},{2,3},{3,4},{4,5},{5,6},{6,7},{8,9},{9,10},{10,11},{11... | collective-permute-start | bytes 196616 | tf_op jit(solution)/shard_map/ppermute | solution.py:13
  13.1 11.6 %collective-permute-start.1 = (f32[8,2048]{1,0:T(8,128)S(1)}, f32[8,2048]{1,0:T(8,128)S(1)}, u32[]{:S(2)}, u32[]{:S(2)}) collective-permute-start(f32[8,2048]{1,0:T(8,128)S(1)} %get-tuple-element.10), channel_id=1, source_target_pairs={{1,0},{2,1},{3,2},{4,3},{5,4},{6,5},{7,6},{9,8},{10,9},{11,10},{12... | collective-permute-start | bytes 196616 | tf_op jit(solution)/shard_map/ppermute | solution.py:14
  15.9 6.2 %collective-permute-start.2 = (bf16[8,2048]{1,0:T(8,128)(2,1)S(1)}, bf16[8,2048]{1,0:T(8,128)(2,1)S(1)}, u32[]{:S(2)}, u32[]{:S(2)}) collective-permute-start(bf16[8,2048]{1,0:T(8,128)(2,1)S(1)} %get-tuple-element.11), channel_id=1, source_target_pairs={{0,1},{1,2},{2,3},{3,4},{4,5},{5,6},{6,7},{8,9},{9,10},{10,11},{11... | collective-permute-start | bytes 98312 | tf_op jit(solution)/shard_map/ppermute | solution.py:13
  19.5 5.2 %collective-permute-start.3 = (bf16[8,2048]{1,0:T(8,128)(2,1)S(1)}, bf16[8,2048]{1,0:T(8,128)(2,1)S(1)}, u32[]{:S(2)}, u32[]{:S(2)}) collective-permute-start(bf16[8,2048]{1,0:T(8,128)(2,1)S(1)} %get-tuple-element.12), channel_id=1, source_target_pairs={{1,0},{2,1},{3,2},{4,3},{5,4},{6,5},{7,6},{9,8},{10,9},{11,10},{12... | collective-permute-start | bytes 98312 | tf_op jit(solution)/shard_map/ppermute | solution.py:14
  84.1 5.5 %slice-start = ((s8[8388608]{0:T(1024)(128)(4,1)}), s8[4194304]{0:T(1024)(128)(4,1)S(1)}, s32[]{:S(2)}) async-start(s8[8388608]{0:T(1024)(128)(4,1)} %bitcast.41), calls=%async_computation.6 | async-start | bytes 8388608
  84.1 6.3 %slice-start.1 = ((s8[8388608]{0:T(1024)(128)(4,1)}), s8[4194304]{0:T(1024)(128)(4,1)S(1)}, s32[]{:S(2)}) async-start(s8[8388608]{0:T(1024)(128)(4,1)} %bitcast.41), calls=%async_computation.7 | async-start | bytes 8388608
  84.1 6.5 %copy-start = (f32[1,128,2048]{2,1,0:T(8,128)S(1)}, f32[1,128,2048]{2,1,0:T(8,128)}, u32[]{:S(2)}) copy-start(f32[1,128,2048]{2,1,0:T(8,128)} %param.10) | copy-start | bytes 3145732
  100.6 1.4 copy-start.1
  103.5 16.1 %all-to-all-start = ((bf16[128,8,256]{2,0,1:T(8,128)(2,1)}), bf16[128,8,256]{2,0,1:T(8,128)(2,1)S(1)}, u32[]{:S(2)}, u32[]{:S(2)}) async-start(bf16[128,8,256]{2,0,1:T(8,128)(2,1)} %bitcast.39), calls=%async_computation | async-start | bytes 1048576 | tf_op jit(solution)/shard_map/all_to_all | solution.py:37
  107.2 91.1 %reduce-scatter.2.cloned.1.call-start = ((), (), s32[]{:S(2)}) async-start(), calls=%async_computation.4 | async-start | bytes 2228224 | tf_op jit(solution)/shard_map/reduce_scatter | solution.py:39
Sparse Core Ops, SparseCore 0:
  10.3 73.7 all-gather.3
  85.8 33.5 all-gather.5
  124.5 73.7 reduce-scatter.1

commit v2 on v1

v2 whole, which is shorter than its diff:
```python
import functools

import jax
import jax.numpy as jnp
from jax import lax
from jax.experimental import pallas as pl
from jax.experimental.pallas import tpu as pltpu
from jax.sharding import PartitionSpec as P

SWEEPS = 8
HALO = 8
SIDE = 4
SLABS = 8
WIDE = 256
BLOCK = 128
F32, BF16 = jnp.float32, jnp.bfloat16


def with_halo(value, size):
    up = [(i, i + 1) for i in range(size - 1)]
    down = [(i + 1, i) for i in range(size - 1)]
    before = lax.ppermute(value[-HALO:], "slab", up)
    after = lax.ppermute(value[:HALO], "slab", down)
    return jnp.concatenate([before, value, after], axis=0)


def place():
    freq, slab = lax.axis_index("freq"), lax.axis_index("slab")
    return freq // SIDE, lax.rem(freq, SIDE), slab


def beyond(me, step, size):
    return lax.rem(me + step, size)


def send(src, dst, sems, index, to):
    copy = pltpu.make_async_remote_copy(
        src_ref=src, dst_ref=dst, send_sem=sems[0].at[index], recv_sem=sems[1].at[index],
        device_id=to, device_id_type=pl.DeviceIdType.MESH,
    )
    copy.start()
    return copy


def tail_kernel(part, every, image, turned, gathered, terms, sent, came, sums, came2, final,
                a2a_s, a2a_r, one_s, one_r, two_s, two_r, end_s, end_r):
    x, y, slab = place()
    freq = x * SIDE + y
    along_x = [{"freq": beyond(x, d, SIDE) * SIDE + y, "slab": slab} for d in range(1, SIDE)]
    along_y = [{"freq": x * SIDE + beyond(y, d, SIDE), "slab": slab} for d in range(1, SIDE)]
    line = [{"freq": freq, "slab": beyond(slab, d, SLABS)} for d in range(1, SLABS)]

    barrier = pltpu.get_barrier_semaphore()
    peers = along_x + along_y + line
    for peer in peers:
        pl.semaphore_signal(barrier, inc=1, device_id=peer, device_id_type=pl.DeviceIdType.MESH)
    for s in range(SLABS):
        turned[s] = part[:, s * WIDE:(s + 1) * WIDE].T
    pl.semaphore_wait(barrier, len(peers))

    lanes = pl.ds(pl.multiple_of(slab * BLOCK, BLOCK), BLOCK)
    copies = []
    for d in range(1, SLABS):
        copies.append(send(turned.at[beyond(slab, d, SLABS)], gathered.at[:, lanes], (a2a_s, a2a_r), d - 1, line[d - 1]))
    gathered[:, lanes] = turned[slab]
    for copy in copies:
        copy.wait()

    for n in range(SIDE):
        term = jnp.dot(gathered[...], every[:, n * 512:(n + 1) * 512], preferred_element_type=F32)
        terms[0, n] = term[:BLOCK]
        sent[0, n] = term[:BLOCK].astype(BF16)
        for m in range(SIDE):
            piece = term[BLOCK:, m * BLOCK:(m + 1) * BLOCK]
            terms[1, m, :, n * BLOCK:(n + 1) * BLOCK] = piece
            sent[1, m, :, n * BLOCK:(n + 1) * BLOCK] = piece.astype(BF16)

    first = []
    for half, (me, ways) in enumerate(((x, along_x), (y, along_y))):
        for d in range(1, SIDE):
            first.append(send(sent.at[half, beyond(me, d, SIDE)], came.at[half, d - 1],
                              (one_s, one_r), half * 3 + d - 1, ways[d - 1]))
    second = []
    for half, (me, other, ways) in enumerate(((x, y, along_y), (y, x, along_x))):
        for d in range(3):
            first[half * 3 + d].wait()
        total = terms[half, me]
        for d in range(3):
            total += came[half, d].astype(F32)
        for m in range(SIDE):
            sums[half, m] = total[:, m * BLOCK:(m + 1) * BLOCK]
        for d in range(1, SIDE):
            second.append(send(sums.at[half, beyond(other, d, SIDE)], came2.at[half, d - 1],
                               (two_s, two_r), half * 3 + d - 1, ways[d - 1]))
    for half, other in enumerate((y, x)):
        for d in range(3):
            second[half * 3 + d].wait()
        total = sums[half, other]
        for d in range(3):
            total += came2[half, d]
        flat = total.T
        for s in range(SLABS):
            final[s, :, half * BLOCK:(half + 1) * BLOCK] = flat[s * 16:(s + 1) * 16]
    here = pl.ds(pl.multiple_of(slab * WIDE, WIDE), WIDE)
    ends = []
    for d in range(1, SLABS):
        ends.append(send(final.at[beyond(slab, d, SLABS)], image.at[:, here], (end_s, end_r), d - 1, line[d - 1]))
    image[:, here] = final[slab]
    for copy in ends:
        copy.wait()


def tail(part, every):
    vmem = pl.BlockSpec(memory_space=pltpu.VMEM)
    dma = pltpu.SemaphoreType.DMA
    return pl.pallas_call(
        tail_kernel,
        name="tail",
        out_shape=jax.ShapeDtypeStruct((16, 2048), F32),
        in_specs=[vmem, vmem],
        out_specs=vmem,
        scratch_shapes=[
            pltpu.VMEM((SLABS, WIDE, BLOCK), BF16),
            pltpu.VMEM((WIDE, SLABS * BLOCK), BF16),
            pltpu.VMEM((2, SIDE, BLOCK, 512), F32),
            pltpu.VMEM((2, SIDE, BLOCK, 512), BF16),
            pltpu.VMEM((2, 3, BLOCK, 512), BF16),
            pltpu.VMEM((2, SIDE, BLOCK, BLOCK), F32),
            pltpu.VMEM((2, 3, BLOCK, BLOCK), F32),
            pltpu.VMEM((SLABS, 16, WIDE), F32),
            dma((7,)), dma((7,)), dma((6,)), dma((6,)), dma((6,)), dma((6,)), dma((7,)), dma((7,)),
        ],
        compiler_params=pltpu.CompilerParams(collective_id=0, has_side_effects=True, vmem_limit_bytes=40 << 20),
    )(part, every)


def shards(fine_model, resample, lateral, shift, source, receiver):
    slabs = lax.axis_size("slab")
    oper = resample[0]
    rows = oper.shape[0]
    every = lax.all_gather(oper, "slab", axis=0, tiled=True)
    wide = with_halo(oper, slabs)
    src = with_halo(source[0], slabs)
    model = lax.all_gather(fine_model, ("freq", "slab"), axis=0, tiled=True)
    coarse = jnp.dot(wide, model, preferred_element_type=F32)
    at = lax.axis_index("slab") * rows - HALO + lax.broadcasted_iota(jnp.int32, (rows + 2 * HALO, 1), 0)
    inside = (at >= 0) & (at < rows * slabs)
    inv = jnp.where(inside, 1.0 / (4.0 + shift[0] * coarse * coarse), 0.0)
    field = src * inv
    for sweep in range(1, SWEEPS):
        padded = jnp.pad(field, ((1, 1), (0, 0)))
        beside = padded[2:] + padded[:-2]
        side = jnp.dot(field.astype(BF16), lateral, preferred_element_type=F32)
        field = (src + 0.5 * beside + side) * inv
    part = (field[HALO:-HALO] * receiver[0]).astype(BF16)
    return tail(part, every)


def solution(mesh):
    in_specs = (
        P(("freq", "slab"), None),
        P("freq", "slab", None),
        P(),
        P("freq"),
        P("freq", "slab", None),
        P("freq", "slab", None),
    )
    out_specs = P(("freq", "slab"), None)
    return jax.shard_map(shards, mesh=mesh, in_specs=in_specs, out_specs=out_specs, check_vma=False)
```

time: 219 us -> 158 us (0.72)
  waiting for transfers between devices: 149 us -> 75.6 us
  Pallas kernels: 0 us -> 31.8 us
  blocking collectives: 11.9 us -> 0 us
  matrix products: 21.2 us -> 16.6 us
  starting transfers between devices: 16.1 us -> 12.4 us
    reduce_scatter x1 -> x0, waiting for transfers between devices: 73.9 us -> none  [shards(): mine = lax.psum_scatter(term, 'freq', scatter_dimension=0, tiled=True)]
    pallas_call x0 -> x1, Pallas kernels: none -> 31.8 us  [tail(): pl.pallas_call(tail_kernel, name='tail', out_shape=jax.ShapeDtypeStruct((...]
    all_to_all x1 -> x0, blocking collectives: 11.9 us -> none  [shards(): return lax.all_to_all(mine, 'slab', split_axis=0, concat_axis=1, tiled=True)]
    dot_general x9 -> x8, matrix products: 21.2 us -> 16.6 us  [the longest x7 11.1 us: shards(): side = jnp.dot(field.astype(BF16), lateral, preferred_element_type=F32)]
    all_to_all x1 -> x0, starting transfers between devices: 3.65 us -> none  [shards(): cols = lax.all_to_all(part, 'slab', split_axis=1, concat_axis=0, tiled=True)]
    unnamed x8 -> x11, local copies, waits for them, and re-layouts: 1.05 us -> 3.9 us
  transfers between devices with their start and end apart: 8 -> 6, of which waited for: 5 -> 3; matrix products, arithmetic and copies ran while one was open for 9% -> 12% of each run, Pallas kernels for 0% -> 0%
where the time goes in v2:
time: 158 us; the launch traced here: 157 us
  waiting for transfers between devices  75.6 us (48%)
  Pallas kernels  31.8 us (20%)
  matrix products  16.6 us (11%)
  between operations  14.2 us (9%)
  starting transfers between devices  12.4 us (8%)
  local copies, waits for them, and re-layouts  5.95 us (4%)
    all_gather x1, waiting for transfers between devices, shards(): model = lax.all_gather(fine_model, ('freq', 'slab'), axis=0, tiled=True)  58.7 us
    pallas_call x1, Pallas kernels, tail(): pl.pallas_call(tail_kernel, name='tail', out_shape=jax.ShapeDtypeStruct((...  31.8 us
    all_gather x1, waiting for transfers between devices, shards(): every = lax.all_gather(oper, 'slab', axis=0, tiled=True)  12.9 us
    dot_general x7, matrix products, shards(): side = jnp.dot(field.astype(BF16), lateral, preferred_element_type=F32)  11.1 us
    ppermute x2, starting transfers between devices, with_halo(): before = lax.ppermute(value[-HALO:], 'slab', up)  8.57 us
    dot_general x1, matrix products, shards(): coarse = jnp.dot(wide, model, preferred_element_type=F32)  5.46 us
    unnamed x11, local copies, waits for them, and re-layouts  3.9 us
    ppermute x2, starting transfers between devices, with_halo(): after = lax.ppermute(value[:HALO], 'slab', down)  3.84 us
  transfers between devices with their start and end apart: 6, of which 3 were waited for; matrix products, arithmetic and copies ran while one was open for 12% of the time, Pallas kernels for 0%

profile of v2, /device:TPU:1, one launch (start us, length us, event | category | flops | bytes accessed | tf_op | source)
XLA Modules:
  0.0 157.2 jit_solution(12269979330939843632)
XLA Ops:
  6.5 0.7 all-gather.4.cloned.1.call-update
  7.3 0.7 all-gather.6.cloned.1.call-update
  8.0 0.9 slice_bitcast_fusion.1
  8.9 4.9 %collective-permute-start = (f32[8,2048]{1,0:T(8,128)S(1)}, f32[8,2048]{1,0:T(8,128)S(1)}, u32[]{:S(2)}, u32[]{:S(2)}) collective-permute-start(f32[8,2048]{1,0:T(8,128)S(1)} %get-tuple-element.9), channel_id=1, source_target_pairs={{0,1},{1,2},{2,3},{3,4},{4,5},{5,6},{6,7},{8,9},{9,10},{10,11},{11... | collective-permute-start | bytes 196616 | tf_op jit(solution)/shard_map/ppermute | solution.py:22
  13.8 1.9 %collective-permute-start.1 = (f32[8,2048]{1,0:T(8,128)S(1)}, f32[8,2048]{1,0:T(8,128)S(1)}, u32[]{:S(2)}, u32[]{:S(2)}) collective-permute-start(f32[8,2048]{1,0:T(8,128)S(1)} %get-tuple-element.10), channel_id=1, source_target_pairs={{1,0},{2,1},{3,2},{4,3},{5,4},{6,5},{7,6},{9,8},{10,9},{11,10},{12... | collective-permute-start | bytes 196616 | tf_op jit(solution)/shard_map/ppermute | solution.py:23
  15.8 0.8 slice_bitcast_fusion.3
  16.6 3.6 %collective-permute-start.2 = (bf16[8,2048]{1,0:T(8,128)(2,1)S(1)}, bf16[8,2048]{1,0:T(8,128)(2,1)S(1)}, u32[]{:S(2)}, u32[]{:S(2)}) collective-permute-start(bf16[8,2048]{1,0:T(8,128)(2,1)S(1)} %get-tuple-element.11), channel_id=1, source_target_pairs={{0,1},{1,2},{2,3},{3,4},{4,5},{5,6},{6,7},{8,9},{9,10},{10,11},{11... | collective-permute-start | bytes 98312 | tf_op jit(solution)/shard_map/ppermute | solution.py:22
  20.2 1.9 %collective-permute-start.3 = (bf16[8,2048]{1,0:T(8,128)(2,1)S(1)}, bf16[8,2048]{1,0:T(8,128)(2,1)S(1)}, u32[]{:S(2)}, u32[]{:S(2)}) collective-permute-start(bf16[8,2048]{1,0:T(8,128)(2,1)S(1)} %get-tuple-element.12), channel_id=1, source_target_pairs={{1,0},{2,1},{3,2},{4,3},{5,4},{6,5},{7,6},{9,8},{10,9},{11,10},{12... | collective-permute-start | bytes 98312 | tf_op jit(solution)/shard_map/ppermute | solution.py:23
  22.8 2.6 %collective-permute-done.3 = bf16[8,2048]{1,0:T(8,128)(2,1)S(1)} collective-permute-done((bf16[8,2048]{1,0:T(8,128)(2,1)S(1)}, bf16[8,2048]{1,0:T(8,128)(2,1)S(1)}, u32[]{:S(2)}, u32[]{:S(2)}) %collective-permute-start.3) | collective-permute-done | bytes 32800 | tf_op jit(solution)/shard_map/ppermute | solution.py:23
  25.4 58.7 %all-gather.4.cloned.1.call-done = bf16[2048,2048]{1,0:T(8,128)(2,1)} async-done(((bf16[16,2048]{1,0:T(8,128)(2,1)}), bf16[2048,2048]{1,0:T(8,128)(2,1)}) %all-gather.4.cloned.1.call-update) | async-done | bytes 8388624 | tf_op jit(solution)/shard_map/all_gather | solution.py:144
  84.1 5.5 %pad_maximum_fusion = (f32[144,2048]{1,0:T(8,128)S(1)}, f32[144,2048]{1,0:T(8,128)S(1)}, f32[144,2048]{1,0:T(8,128)S(1)}) fusion(f32[8,2048]{1,0:T(8,128)S(1)} %collective-permute-done.1, f32[128,2048]{1,0:T(8,128)} %bitcast.26, f32[8,2048]{1,0:T(8,128)S(1)} %collective-permute-done, bf16[2048,2048]{1,0:T(8,128)(2,1)} %all-gather.4.cloned.1.call-done, ...), kind=kOutput, calls=%fused_computation.48 | convolution fusion | flops 1212088320 | bytes 13697172 | tf_op jit(solution)/shard_map/dot_general | solution.py:145
  89.6 0.8 slice-done.1
  90.7 1.6 %fusion.4 = f32[144,2048]{1,0:T(8,128)S(1)} fusion(f32[144,2048]{1,0:T(8,128)S(1)} %get-tuple-element.13, f32[144,2048]{1,0:T(8,128)S(1)} %get-tuple-element.8, bf16[2048,2048]{1,0:T(8,128)(2,1)S(1)} %bitcast.25, f32[8,2048]{1,0:T(8,128)S(1)} %collective-permute-done.1, f32[128,2048]{1,0:T(8,128)S(1)} %bitcast.27, f32[8,2048]{1,0:T(8,128)S(1)} %collective-permute-done), kind=kOutput, calls=%fused_computation.19 | convolution fusion | flops 1210318848 | bytes 14286848 | tf_op jit(solution)/shard_map/dot_general | solution.py:153
  92.2 1.6 %fusion.9 = f32[144,2048]{1,0:T(8,128)S(1)} fusion(f32[144,2048]{1,0:T(8,128)S(1)} %get-tuple-element.13, f32[144,2048]{1,0:T(8,128)S(1)} %fusion.4, bf16[2048,2048]{1,0:T(8,128)(2,1)S(1)} %bitcast.25, f32[8,2048]{1,0:T(8,128)S(1)} %collective-permute-done.1, f32[128,2048]{1,0:T(8,128)S(1)} %bitcast.28, f32[8,2048]{1,0:T(8,128)S(1)} %collective-permute-done), kind=kOutput, calls=%fused_computation.24 | convolution fusion | flops 1210318848 | bytes 14286848 | tf_op jit(solution)/shard_map/dot_general | solution.py:153
  93.8 1.6 %fusion.14 = f32[144,2048]{1,0:T(8,128)S(1)} fusion(f32[144,2048]{1,0:T(8,128)S(1)} %get-tuple-element.13, f32[144,2048]{1,0:T(8,128)S(1)} %fusion.9, bf16[2048,2048]{1,0:T(8,128)(2,1)S(1)} %bitcast.25, f32[8,2048]{1,0:T(8,128)S(1)} %collective-permute-done.1, f32[128,2048]{1,0:T(8,128)S(1)} %bitcast.29, f32[8,2048]{1,0:T(8,128)S(1)} %collective-permute-done), kind=kOutput, calls=%fused_computation.29 | convolution fusion | flops 1210318848 | bytes 14286848 | tf_op jit(solution)/shard_map/dot_general | solution.py:153
  95.4 1.6 %fusion.19 = f32[144,2048]{1,0:T(8,128)S(1)} fusion(f32[144,2048]{1,0:T(8,128)S(1)} %get-tuple-element.13, f32[144,2048]{1,0:T(8,128)S(1)} %fusion.14, bf16[2048,2048]{1,0:T(8,128)(2,1)S(1)} %bitcast.25, f32[8,2048]{1,0:T(8,128)S(1)} %collective-permute-done.1, f32[128,2048]{1,0:T(8,128)S(1)} %bitcast.30, f32[8,2048]{1,0:T(8,128)S(1)} %collective-permute-done), kind=kOutput, calls=%fused_computation.34 | convolution fusion | flops 1210318848 | bytes 14286848 | tf_op jit(solution)/shard_map/dot_general | solution.py:153
  97.0 1.6 %fusion.24 = f32[144,2048]{1,0:T(8,128)S(1)} fusion(f32[144,2048]{1,0:T(8,128)S(1)} %get-tuple-element.13, f32[144,2048]{1,0:T(8,128)S(1)} %fusion.19, bf16[2048,2048]{1,0:T(8,128)(2,1)S(1)} %bitcast.25, f32[8,2048]{1,0:T(8,128)S(1)} %collective-permute-done.1, f32[128,2048]{1,0:T(8,128)S(1)} %bitcast.31, f32[8,2048]{1,0:T(8,128)S(1)} %collective-permute-done), kind=kOutput, calls=%fused_computation.39 | convolution fusion | flops 1210318848 | bytes 14286848 | tf_op jit(solution)/shard_map/dot_general | solution.py:153
  98.6 1.6 %fusion.29 = f32[144,2048]{1,0:T(8,128)S(1)} fusion(f32[144,2048]{1,0:T(8,128)S(1)} %get-tuple-element.13, f32[144,2048]{1,0:T(8,128)S(1)} %fusion.24, bf16[2048,2048]{1,0:T(8,128)(2,1)S(1)} %bitcast.25, f32[8,2048]{1,0:T(8,128)S(1)} %collective-permute-done.1, f32[128,2048]{1,0:T(8,128)S(1)} %bitcast.32, f32[8,2048]{1,0:T(8,128)S(1)} %collective-permute-done), kind=kOutput, calls=%fused_computation.44 | convolution fusion | flops 1210318848 | bytes 14286848 | tf_op jit(solution)/shard_map/dot_general | solution.py:153
  100.7 1.6 %fusion.44 = f32[144,2048]{1,0:T(8,128)S(1)} fusion(bf16[2048,2048]{1,0:T(8,128)(2,1)S(1)} %bitcast.25, f32[144,2048]{1,0:T(8,128)S(1)} %fusion.29), kind=kOutput, calls=%fused_computation.62 | convolution fusion | flops 1208254464 | bytes 10747904 | tf_op jit(solution)/shard_map/dot_general | solution.py:153
  102.3 0.6 fusion.34.part
  102.9 12.9 %all-gather.6.cloned.1.call-done = bf16[1,1024,2048]{2,1,0:T(8,128)(2,1)} async-done(((bf16[1,128,2048]{2,1,0:T(8,128)(2,1)}), bf16[1,1024,2048]{2,1,0:T(8,128)(2,1)}) %all-gather.6.cloned.1.call-update) | async-done | bytes 4194320 | tf_op jit(solution)/shard_map/all_gather | solution.py:141
  115.7 2.2 %copy-done = bf16[1,1024,2048]{2,1,0:T(8,128)(2,1)S(1)} copy-done((bf16[1,1024,2048]{2,1,0:T(8,128)(2,1)S(1)}, bf16[1,1024,2048]{2,1,0:T(8,128)(2,1)}, u32[]{:S(2)}) %copy-start) | copy-done | bytes 4194328
  117.9 31.8 %tail.1 = f32[16,2048]{1,0:T(8,128)S(1)} custom-call(bf16[128,2048]{1,0:T(8,128)(2,1)S(1)} %fusion.34.part, bf16[1024,2048]{1,0:T(8,128)(2,1)S(1)} %bitcast.23), custom_call_target="tpu_custom_call" | custom-call | tf_op jit(solution)/shard_map/tail/pallas_call | solution.py:116
  149.7 0.7 copy.9
  (16 shorter events, 0.7 us)
Async XLA Ops:
  6.5 77.6 %all-gather.4.cloned.1.call-start = ((), (), s32[]{:S(2)}) async-start(), calls=%async_computation | async-start | bytes 8454144 | tf_op jit(solution)/shard_map/all_gather | solution.py:144
  7.3 108.5 %all-gather.6.cloned.1.call-start = ((), (), s32[]{:S(2)}) async-start(), calls=%async_computation.1 | async-start | bytes 4718592 | tf_op jit(solution)/shard_map/all_gather | solution.py:141
  8.9 16.5 %collective-permute-start = (f32[8,2048]{1,0:T(8,128)S(1)}, f32[8,2048]{1,0:T(8,128)S(1)}, u32[]{:S(2)}, u32[]{:S(2)}) collective-permute-start(f32[8,2048]{1,0:T(8,128)S(1)} %get-tuple-element.9), channel_id=1, source_target_pairs={{0,1},{1,2},{2,3},{3,4},{4,5},{5,6},{6,7},{8,9},{9,10},{10,11},{11... | collective-permute-start | bytes 196616 | tf_op jit(solution)/shard_map/ppermute | solution.py:22
  13.8 11.6 %collective-permute-start.1 = (f32[8,2048]{1,0:T(8,128)S(1)}, f32[8,2048]{1,0:T(8,128)S(1)}, u32[]{:S(2)}, u32[]{:S(2)}) collective-permute-start(f32[8,2048]{1,0:T(8,128)S(1)} %get-tuple-element.10), channel_id=1, source_target_pairs={{1,0},{2,1},{3,2},{4,3},{5,4},{6,5},{7,6},{9,8},{10,9},{11,10},{12... | collective-permute-start | bytes 196616 | tf_op jit(solution)/shard_map/ppermute | solution.py:23
  16.6 6.2 %collective-permute-start.2 = (bf16[8,2048]{1,0:T(8,128)(2,1)S(1)}, bf16[8,2048]{1,0:T(8,128)(2,1)S(1)}, u32[]{:S(2)}, u32[]{:S(2)}) collective-permute-start(bf16[8,2048]{1,0:T(8,128)(2,1)S(1)} %get-tuple-element.11), channel_id=1, source_target_pairs={{0,1},{1,2},{2,3},{3,4},{4,5},{5,6},{6,7},{8,9},{9,10},{10,11},{11... | collective-permute-start | bytes 98312 | tf_op jit(solution)/shard_map/ppermute | solution.py:22
  20.2 5.2 %collective-permute-start.3 = (bf16[8,2048]{1,0:T(8,128)(2,1)S(1)}, bf16[8,2048]{1,0:T(8,128)(2,1)S(1)}, u32[]{:S(2)}, u32[]{:S(2)}) collective-permute-start(bf16[8,2048]{1,0:T(8,128)(2,1)S(1)} %get-tuple-element.12), channel_id=1, source_target_pairs={{1,0},{2,1},{3,2},{4,3},{5,4},{6,5},{7,6},{9,8},{10,9},{11,10},{12... | collective-permute-start | bytes 98312 | tf_op jit(solution)/shard_map/ppermute | solution.py:23
  84.1 5.5 %slice-start = ((s8[8388608]{0:T(1024)(128)(4,1)}), s8[4194304]{0:T(1024)(128)(4,1)S(1)}, s32[]{:S(2)}) async-start(s8[8388608]{0:T(1024)(128)(4,1)} %bitcast.24), calls=%async_computation.2 | async-start | bytes 8388608
  84.1 6.3 %slice-start.1 = ((s8[8388608]{0:T(1024)(128)(4,1)}), s8[4194304]{0:T(1024)(128)(4,1)S(1)}, s32[]{:S(2)}) async-start(s8[8388608]{0:T(1024)(128)(4,1)} %bitcast.24), calls=%async_computation.3 | async-start | bytes 8388608
  84.1 6.5 %copy-start.1 = (f32[1,128,2048]{2,1,0:T(8,128)S(1)}, f32[1,128,2048]{2,1,0:T(8,128)}, u32[]{:S(2)}) copy-start(f32[1,128,2048]{2,1,0:T(8,128)} %param.10) | copy-start | bytes 3145732
  100.6 1.6 %copy-start.2 = (f32[1,128,2048]{2,1,0:T(8,128)S(1)}, f32[1,128,2048]{2,1,0:T(8,128)}, u32[]{:S(2)}) copy-start(f32[1,128,2048]{2,1,0:T(8,128)} %param.11) | copy-start | bytes 3145732
  115.7 2.2 %copy-start = (bf16[1,1024,2048]{2,1,0:T(8,128)(2,1)S(1)}, bf16[1,1024,2048]{2,1,0:T(8,128)(2,1)}, u32[]{:S(2)}) copy-start(bf16[1,1024,2048]{2,1,0:T(8,128)(2,1)} %all-gather.6.cloned.1.call-done) | copy-start | bytes 12582916
Sparse Core Ops, SparseCore 0:
  10.3 73.7 all-gather.3
  85.8 29.8 all-gather.5

commit v3 on v1

v3 whole, which is shorter than its diff:
```python
import functools

import jax
import jax.numpy as jnp
from jax import lax
from jax.experimental import pallas as pl
from jax.experimental.pallas import tpu as pltpu
from jax.sharding import PartitionSpec as P

SWEEPS = 8
HALO = 8
SIDE = 4
SLABS = 8
ROWS = 128
TALL = ROWS + 2 * HALO
CHIP = 2 * ROWS
NL = 2048
HALF = NL // 2
PATH = HALF // 2
WIDE = NL // SLABS
BLOCK = 128
F32, BF16 = jnp.float32, jnp.bfloat16
MESH = pl.DeviceIdType.MESH


def turn(value, size):
    return lax.rem(value, size)


def ds(start, size, multiple=128):
    return pl.ds(pl.multiple_of(start, multiple), size)


class Links:
    def __init__(self, send, recv):
        self.send, self.recv, self.used, self.all = send, recv, 0, []

    def start(self, src, dst, to):
        copy = pltpu.make_async_remote_copy(
            src_ref=src, dst_ref=dst, send_sem=self.send.at[self.used], recv_sem=self.recv.at[self.used],
            device_id=to, device_id_type=MESH,
        )
        copy.start()
        self.used += 1
        self.all.append(copy)
        return copy

    def finish(self):
        for copy in self.all:
            copy.wait_send()


def migrate(fine, oper, lateral, shift, source, receiver, image,
            fa, fb, lhs, edge, every, lat, src, rec, invc, inv, field, narrow,
            turned, gathered, terms, sent, came, sums, came2, final, send_sem, recv_sem, local_sem):
    freq, slab = lax.axis_index("freq"), lax.axis_index("slab")
    x, y, z, core = freq // SIDE, turn(freq, SIDE), slab // 2, turn(slab, 2)
    other = 1 - core

    def at(dx=0, dy=0, dz=0, dc=0):
        return {"freq": turn(x + dx, SIDE) * SIDE + turn(y + dy, SIDE),
                "slab": turn(z + dz, SIDE) * 2 + turn(core + dc, 2)}

    links = Links(send_sem, recv_sem)
    line = [{"freq": freq, "slab": turn(slab + d, SLABS)} for d in range(1, SLABS)]

    here = ds(slab * ROWS, ROWS)
    mine = ds(core * 16, 16, 16)
    local = {}
    for name, a, b in (
        ("fa", fine.at[:, ds(core * HALF, PATH)], fa.at[x, y, z, mine]),
        ("fb", fine.at[:, ds(core * HALF + PATH, PATH)], fb.at[x, y, z, mine]),
        ("lhs", oper, lhs.at[ds(core * ROWS, ROWS)]),
        ("every", oper, every.at[here]),
        ("src", source, src.at[HALO:HALO + ROWS]),
        ("lat", lateral, lat),
        ("rec", receiver, rec),
    ):
        local[name] = pltpu.make_async_copy(a, b, local_sem.at[len(local)])
        local[name].start()

    barrier = pltpu.get_barrier_semaphore()
    peers = line + [at(dx=d, dc=e) for d in (1, 2, 3) for e in (0, 1)] + [at(dy=d, dc=e) for d in (1, 2, 3) for e in (0, 1)]
    for peer in peers:
        pl.semaphore_signal(barrier, inc=1, device_id=peer, device_id_type=MESH)
    pl.semaphore_wait(barrier, len(peers))

    one = {0: [], 1: []}
    for d in range(SIDE):
        for e in range(2):
            if d or e:
                column = turn(core + e, 2) * HALF
                one[0].append(links.start(fine.at[:, ds(column, PATH)], fa.at[x, y, z, mine], at(dy=d, dc=e)))
                one[1].append(links.start(fine.at[:, ds(column + PATH, PATH)], fb.at[x, y, z, mine], at(dx=d, dc=e)))
    rows = links.start(oper, lhs.at[ds(core * ROWS, ROWS)], at(dc=1))
    early = []
    for e in range(2):
        to = {"freq": freq, "slab": turn(z + 3 - 2 * core, SIDE) * 2 + turn(core + e, 2)}
        early.append(links.start(oper.at[ds(core * (ROWS - 16), 16, 16)], edge.at[other], to))
    late = [
        links.start(source.at[ROWS - HALO:ROWS], src.at[0:HALO], line[0]),
        links.start(source.at[0:HALO], src.at[HALO + ROWS:TALL], line[SLABS - 2]),
    ]

    def chunk(path, step, k):
        if path == 0:
            return fa.at[turn(x + step, SIDE), :, turn(z + k, SIDE)]
        return fb.at[:, turn(y + step, SIDE), turn(z + k, SIDE)]

    def ahead(path, step):
        return at(dx=step) if path == 0 else at(dy=step)

    order = (0, 3, 1, 2)
    two, three, passed = {}, {}, {}

    def spread(path, k):
        part = chunk(path, 0, order[k])
        three[path, k] = (links.start(part, part, ahead(path, 1)), links.start(part, part, ahead(path, 3)))

    def forward(path, k):
        if k < 2:
            three[path, k][0].wait_recv()
            part = chunk(path, 3, order[k])
            passed[path, k] = links.start(part, part, ahead(path, 1))
        else:
            three[path, k][1].wait_recv()
            part = chunk(path, 1, order[k])
            passed[path, k] = links.start(part, part, ahead(path, 3))

    for path in (0, 1):
        local["fa" if path == 0 else "fb"].wait()
        for copy in one[path]:
            copy.wait_recv()
        part = chunk(path, 0, 0)
        for k in (1, 2, 3):
            two[path, k] = links.start(part, part, at(dz=SIDE - order[k]))
        spread(path, 0)
    for k in (1, 2):
        for path in (0, 1):
            two[path, k].wait_recv()
            spread(path, k)
    for path in (0, 1):
        forward(path, 0)
    for path in (0, 1):
        two[path, 3].wait_recv()
        spread(path, 3)

    local["every"].wait()
    whole = every.at[here]
    beside_core = links.start(whole, whole, at(dc=1))
    along = (links.start(whole, whole, at(dz=1)), links.start(whole, whole, at(dz=3)))

    for k in (1, 2, 3):
        for path in (0, 1):
            forward(path, k)

    for copy in early:
        copy.wait_recv()
    lhs[CHIP:CHIP + HALO] = edge[0, 16 - HALO:16]
    lhs[CHIP + HALO:CHIP + 2 * HALO] = edge[1, 0:HALO]
    local["lhs"].wait()
    rows.wait_recv()
    swapped = []
    for path, model in ((0, fa), (1, fb)):
        for k in range(SIDE):
            three[path, k][1 if k < 2 else 0].wait_recv()
            passed[path, k].wait_recv()
        columns = slice(path * PATH, (path + 1) * PATH)
        coarse = jnp.dot(lhs[...], model[...].reshape(NL, PATH), preferred_element_type=F32)
        part = 1.0 / (4.0 + shift[0] * coarse * coarse)
        invc[HALO:HALO + CHIP, columns] = part[:CHIP]
        invc[0:HALO, columns] = jnp.where(z > 0, part[CHIP:CHIP + HALO], 0.0)
        invc[HALO + CHIP:, columns] = jnp.where(z < SIDE - 1, part[CHIP + HALO:], 0.0)
        to = ds(core * HALF + path * PATH, PATH)
        swapped.append(links.start(invc.at[ds(other * ROWS, TALL), columns], inv.at[:, to], at(dc=1)))
        inv[:, to] = invc[ds(core * ROWS, TALL), columns]

    local["src"].wait()
    for copy in late + swapped:
        copy.wait_recv()
    for n in range(SIDE):
        columns = slice(n * 512, (n + 1) * 512)
        value = src[:, columns] * inv[:, columns]
        field[0, :, columns] = value
        narrow[0, :, columns] = value.astype(BF16)
    local["lat"].wait()
    local["rec"].wait()
    forwarded, crossed = [], []
    for sweep in range(1, SWEEPS):
        old, new = (sweep - 1) % 2, sweep % 2
        for n in range(SIDE):
            columns = slice(n * 512, (n + 1) * 512)
            side = jnp.dot(narrow[old], lat[:, columns], preferred_element_type=F32)
            before = field[old, :, columns]
            beside = pltpu.roll(before, 1, 0) + pltpu.roll(before, TALL - 1, 0)
            value = (src[:, columns] + 0.5 * beside + side) * inv[:, columns]
            if sweep < SWEEPS - 1:
                field[new, :, columns] = value
                narrow[new, :, columns] = value.astype(BF16)
            else:
                part = value[HALO:HALO + ROWS] * rec[:, columns]
                for m in range(2):
                    turned[2 * n + m] = part[:, m * WIDE:(m + 1) * WIDE].T.astype(BF16)
        if sweep == 2:
            along[0].wait_recv()
            block = turn(z + 3, SIDE) * 2 + core
            part = every.at[ds(block * ROWS, ROWS // 2, 64)]
            forwarded.append(links.start(part, part, at(dz=1)))
            part = every.at[ds(block * ROWS, ROWS)]
            crossed.append(links.start(part, part, at(dc=1)))
            along[1].wait_recv()
            block = turn(z + 1, SIDE) * 2 + core
            part = every.at[ds(block * ROWS + ROWS // 2, ROWS // 2, 64)]
            forwarded.append(links.start(part, part, at(dz=3)))
            part = every.at[ds(block * ROWS, ROWS)]
            crossed.append(links.start(part, part, at(dc=1)))
        if sweep == 6:
            for copy in forwarded:
                copy.wait_recv()
            block = turn(z + 2, SIDE) * 2 + core
            part = every.at[ds(block * ROWS, ROWS)]
            crossed.append(links.start(part, part, at(dc=1)))

    copies = []
    for d in range(1, SLABS):
        copies.append(links.start(turned.at[turn(slab + d, SLABS)], gathered.at[:, here], line[d - 1]))
    gathered[:, here] = turned[slab]
    beside_core.wait_recv()
    for copy in crossed + copies:
        copy.wait_recv()

    for n in range(SIDE):
        term = jnp.dot(gathered[...], every[:, n * 512:(n + 1) * 512], preferred_element_type=F32)
        terms[0, n] = term[:BLOCK]
        sent[0, n] = term[:BLOCK].astype(BF16)
        for m in range(SIDE):
            piece = term[BLOCK:, m * BLOCK:(m + 1) * BLOCK]
            terms[1, m, :, n * BLOCK:(n + 1) * BLOCK] = piece
            sent[1, m, :, n * BLOCK:(n + 1) * BLOCK] = piece.astype(BF16)
    first, second = {}, {}
    for half, me in ((0, x), (1, y)):
        for d in range(1, SIDE):
            first[half, d] = links.start(sent.at[half, turn(me + d, SIDE)], came.at[half, d - 1], ahead(half, d))
    for half, me, it in ((0, x, y), (1, y, x)):
        total = terms[half, me]
        for d in range(1, SIDE):
            first[half, d].wait_recv()
            total += came[half, d - 1].astype(F32)
        for m in range(SIDE):
            sums[half, m] = total[:, m * BLOCK:(m + 1) * BLOCK]
        for d in range(1, SIDE):
            second[half, d] = links.start(sums.at[half, turn(it + d, SIDE)], came2.at[half, d - 1], ahead(1 - half, d))
    for half, it in ((0, y), (1, x)):
        total = sums[half, it]
        for d in range(1, SIDE):
            second[half, d].wait_recv()
            total += came2[half, d - 1]
        flat = total.T
        for s in range(SLABS):
            final[s, :, half * BLOCK:(half + 1) * BLOCK] = flat[s * 16:(s + 1) * 16]
    to = ds(slab * WIDE, WIDE)
    ends = []
    for d in range(1, SLABS):
        ends.append(links.start(final.at[turn(slab + d, SLABS)], image.at[:, to], line[d - 1]))
    image[:, to] = final[slab]
    for copy in ends:
        copy.wait_recv()
    links.finish()


COPIES = 96


def shards(fine_model, resample, lateral, shift, source, receiver):
    anywhere = pl.BlockSpec(memory_space=pl.ANY)
    vmem, dma = pltpu.VMEM, pltpu.SemaphoreType.DMA
    return pl.pallas_call(
        migrate,
        name="migrate",
        out_shape=jax.ShapeDtypeStruct((16, NL), F32),
        in_specs=[anywhere, anywhere, anywhere, pl.BlockSpec(memory_space=pltpu.SMEM), anywhere, anywhere],
        out_specs=pl.BlockSpec(memory_space=pltpu.VMEM),
        scratch_shapes=[
            vmem((SIDE, SIDE, SIDE, 32, PATH), BF16),
            vmem((SIDE, SIDE, SIDE, 32, PATH), BF16),
            vmem((CHIP + 2 * HALO, NL), BF16),
            vmem((2, 16, NL), BF16),
            vmem((SLABS * ROWS, NL), BF16),
            vmem((NL, NL), BF16),
            vmem((TALL, NL), F32),
            vmem((ROWS, NL), F32),
            vmem((CHIP + 2 * HALO, HALF), F32),
            vmem((TALL, NL), F32),
            vmem((2, TALL, NL), F32),
            vmem((2, TALL, NL), BF16),
            vmem((SLABS, WIDE, BLOCK), BF16),
            vmem((WIDE, SLABS * BLOCK), BF16),
            vmem((2, SIDE, BLOCK, 512), F32),
            vmem((2, SIDE, BLOCK, 512), BF16),
            vmem((2, 3, BLOCK, 512), BF16),
            vmem((2, SIDE, BLOCK, BLOCK), F32),
            vmem((2, 3, BLOCK, BLOCK), F32),
            vmem((SLABS, 16, WIDE), F32),
            dma((COPIES,)), dma((COPIES,)), dma((7,)),
        ],
        compiler_params=pltpu.CompilerParams(collective_id=0, has_side_effects=True, vmem_limit_bytes=56 << 20),
    )(fine_model, resample[0], lateral, shift, source[0], receiver[0])


def solution(mesh):
    in_specs = (
        P(("freq", "slab"), None),
        P("freq", "slab", None),
        P(),
        P("freq"),
        P("freq", "slab", None),
        P("freq", "slab", None),
    )
    out_specs = P(("freq", "slab"), None)
    return jax.shard_map(shards, mesh=mesh, in_specs=in_specs, out_specs=out_specs, check_vma=False)
```

time: 219 us -> 85.2 us (0.39)
  waiting for transfers between devices: 149 us -> 0 us
  Pallas kernels: 0 us -> 82.8 us
  matrix products: 21.2 us -> 0 us
  starting transfers between devices: 16.1 us -> 0 us
  between operations: 13.9 us -> 0.66 us
  blocking collectives: 11.9 us -> 0 us
  local copies, waits for them, and re-layouts: 5.6 us -> 1.57 us
    pallas_call x0 -> x1, Pallas kernels: none -> 82.8 us  [shards(): pl.pallas_call(migrate, name='migrate', out_shape=jax.ShapeDtypeStruct((1...]
    reduce_scatter x1 -> x0, waiting for transfers between devices: 73.9 us -> none  [shards(): mine = lax.psum_scatter(term, 'freq', scatter_dimension=0, tiled=True)]
    all_gather x2 -> x0, waiting for transfers between devices: 71.6 us -> none  [the longest x1 59.4 us: shards(): model = lax.all_gather(fine_model, ('freq', 'slab'), axis=0, tiled=True)]
    dot_general x9 -> x0, matrix products: 21.2 us -> none  [the longest x7 10.9 us: shards(): jnp.dot(field.astype(jnp.bfloat16), lateral, preferred_element_type=jnp.f...]
    ppermute x4 -> x0, starting transfers between devices: 12.4 us -> none  [the longest x2 8.57 us: with_halo(): before = lax.ppermute(value[-HALO:], 'slab', up)]
    all_to_all x1 -> x0, blocking collectives: 11.9 us -> none  [shards(): return lax.all_to_all(mine, 'slab', split_axis=0, concat_axis=1, tiled=True)]
    all_to_all x1 -> x0, starting transfers between devices: 3.65 us -> none  [shards(): cols = lax.all_to_all(part, 'slab', split_axis=1, concat_axis=0, tiled=True)]
    ppermute x4 -> x0, waiting for transfers between devices: 2.64 us -> none  [the longest x2 2.63 us: with_halo(): after = lax.ppermute(value[:HALO], 'slab', down)]
  transfers between devices with their start and end apart: 8 -> 0, of which waited for: 5 -> 0; matrix products, arithmetic and copies ran while one was open for 9% -> 0% of each run, Pallas kernels for 0% -> 0%
where the time goes in v3:
time: 85.2 us; the launch traced here: 85 us
  Pallas kernels  82.8 us (97%)
  local copies, waits for them, and re-layouts  1.57 us (2%)
    pallas_call x1, Pallas kernels, shards(): pl.pallas_call(migrate, name='migrate', out_shape=jax.ShapeDtypeStruct((1...  82.8 us

profile of v3, /device:TPU:1, one launch (start us, length us, event | category | flops | bytes accessed | tf_op | source)
XLA Modules:
  0.0 85.0 jit_solution(3884108912308506948)
XLA Ops:
  0.7 82.8 %migrate.1 = f32[16,2048]{1,0:T(8,128)} custom-call(bf16[16,2048]{1,0:T(8,128)(2,1)} %fine.1, bf16[128,2048]{1,0:T(8,128)(2,1)} %bitcast.5, bf16[2048,2048]{1,0:T(8,128)(2,1)} %lateral.1, f32[1]{0:T(128)S(6)} %copy.8.shift, f32[128,2048]{1,0:T(8,128)} %bitcast.3, f32[128,2048]{1,0:T(8,128)} %bitcast.4), custom_call_target="tpu_custom_call" | custom-call | tf_op jit(solution)/shard_map/migrate/pallas_call | solution.py:277
  83.5 1.6 %copy.9 = f32[16,2048]{1,0:T(8,128)} copy(f32[16,2048]{1,0:T(8,128)} %migrate.1) | data formatting | bytes 262144

commit v4 on v3

v4 whole, which is shorter than its diff:
```python
import functools

import jax
import jax.numpy as jnp
from jax import lax
from jax.experimental import pallas as pl
from jax.experimental.pallas import tpu as pltpu
from jax.sharding import PartitionSpec as P

SWEEPS = 8
HALO = 8
SIDE = 4
SLABS = 8
ROWS = 128
TALL = ROWS + 2 * HALO
CHIP = 2 * ROWS
NL = 2048
HALF = NL // 2
PATHS = (((1, 2, 0), 0, 384), ((2, 0, 1), 384, 384), ((0, 1, 2), 768, 256))
WIDE = NL // SLABS
BLOCK = 128
F32, BF16 = jnp.float32, jnp.bfloat16
MESH = pl.DeviceIdType.MESH


def turn(value, size):
    return lax.rem(value, size)


def ds(start, size, multiple=128):
    return pl.ds(pl.multiple_of(start, multiple), size)


class Links:
    def __init__(self, send, recv):
        self.send, self.recv, self.used, self.all = send, recv, 0, []

    def start(self, src, dst, to):
        copy = pltpu.make_async_remote_copy(
            src_ref=src, dst_ref=dst, send_sem=self.send.at[self.used], recv_sem=self.recv.at[self.used],
            device_id=to, device_id_type=MESH,
        )
        copy.start()
        self.used += 1
        self.all.append(copy)
        return copy

    def finish(self):
        for copy in self.all:
            copy.wait_send()


def migrate(fine, oper, lateral, shift, source, receiver, image,
            fa, fb, fc, lhs, edge, every, lat, src, rec, partial, invc, inv, field, narrow,
            turned, gathered, own, sent, came, sums, came2, final, send_sem, recv_sem, local_sem):
    freq, slab = lax.axis_index("freq"), lax.axis_index("slab")
    x, y, z, core = freq // SIDE, turn(freq, SIDE), slab // 2, turn(slab, 2)
    other = 1 - core

    def at(dx=0, dy=0, dz=0, dc=0):
        return {"freq": turn(x + dx, SIDE) * SIDE + turn(y + dy, SIDE),
                "slab": turn(z + dz, SIDE) * 2 + turn(core + dc, 2)}

    links = Links(send_sem, recv_sem)
    line = [{"freq": freq, "slab": turn(slab + d, SLABS)} for d in range(1, SLABS)]

    here = ds(slab * ROWS, ROWS)
    mine = ds(core * 16, 16, 16)
    local = {}
    for name, a, b in (
        (0, fine.at[:, ds(core * HALF, 384)], fa.at[x, y, z, mine]),
        (1, fine.at[:, ds(core * HALF + 384, 384)], fb.at[x, y, z, mine]),
        (2, fine.at[:, ds(core * HALF + 768, 256)], fc.at[x, y, z, mine]),
        ("lhs", oper, lhs.at[ds(core * ROWS, ROWS)]),
        ("every", oper, every.at[here]),
        ("src", source, src.at[HALO:HALO + ROWS]),
        ("lat", lateral, lat),
        ("rec", receiver, rec),
    ):
        local[name] = pltpu.make_async_copy(a, b, local_sem.at[len(local)])
        local[name].start()

    barrier = pltpu.get_barrier_semaphore()
    peers = line + [at(dx=d, dc=e) for d in (1, 2, 3) for e in (0, 1)] + [at(dy=d, dc=e) for d in (1, 2, 3) for e in (0, 1)]
    for peer in peers:
        pl.semaphore_signal(barrier, inc=1, device_id=peer, device_id_type=MESH)
    pl.semaphore_wait(barrier, len(peers))

    models = (fa, fb, fc)

    def along(axis, step, dc=0):
        return at(**{("dx", "dy", "dz")[axis]: step, "dc": dc})

    one, two, three, passed = {}, {}, {}, {}
    for path, (axes, first, size) in enumerate(PATHS):
        one[path] = [
            links.start(fine.at[:, ds(turn(core + e, 2) * HALF + first, size)], models[path].at[x, y, z, mine],
                        along(axes[0], d, e))
            for d in range(SIDE) for e in range(2) if d or e
        ]
    lined = []

    def part_of(block, quarter, quarters=1):
        return every.at[ds(block * ROWS + quarter * 32, 32 * quarters, 32)]

    def lend():
        part = part_of(slab, len(lined))
        lined.append((links.start(part, part, at(dz=1)), links.start(part, part, at(dz=3))))

    local["every"].wait()
    lend()
    order = (0, 3, 1, 2)

    def chunk(path, step, k, of_first=slice(None)):
        where = [x, y, z]
        axes = PATHS[path][0]
        where[axes[0]] = of_first
        where[axes[1]] = turn(where[axes[1]] + order[k], SIDE)
        where[axes[2]] = turn(where[axes[2]] + step, SIDE)
        return models[path].at[tuple(where)]

    def spread(path, k):
        part, axis = chunk(path, 0, k), PATHS[path][0][2]
        three[path, k] = (links.start(part, part, along(axis, 1)), links.start(part, part, along(axis, 3)))

    def forward(path, k):
        axis = PATHS[path][0][2]
        passed[path, k] = []
        for side, (came_from, to, of_first) in enumerate(((3, 1, slice(0, 2)), (1, 3, slice(2, 4)))):
            three[path, k][side].wait_recv()
            part = chunk(path, came_from, k, of_first)
            passed[path, k].append(links.start(part, part, along(axis, to)))

    every_path = range(len(PATHS))
    for path in every_path:
        local[path].wait()
        for copy in one[path]:
            copy.wait_recv()
        part, axis = chunk(path, 0, 0), PATHS[path][0][1]
        for k in (1, 2, 3):
            two[path, k] = links.start(part, part, along(axis, SIDE - order[k]))
            if k == 2:
                spread(path, 0)
    rows = links.start(oper, lhs.at[ds(core * ROWS, ROWS)], at(dc=1))
    early = []
    for e in range(2):
        to = {"freq": freq, "slab": turn(z + 3 - 2 * core, SIDE) * 2 + turn(core + e, 2)}
        early.append(links.start(oper.at[ds(core * (ROWS - 16), 16, 16)], edge.at[other], to))
    late = [
        links.start(source.at[ROWS - HALO:ROWS], src.at[0:HALO], line[0]),
        links.start(source.at[0:HALO], src.at[HALO + ROWS:TALL], line[SLABS - 2]),
    ]
    beside_core = links.start(every.at[here], every.at[here], at(dc=1))
    for k in (1, 2):
        for path in every_path:
            two[path, k].wait_recv()
            spread(path, k)
    for path in every_path:
        forward(path, 0)
    for path in every_path:
        two[path, 3].wait_recv()
        spread(path, 3)
    lend()
    for k in (1, 2, 3):
        for path in every_path:
            forward(path, k)
    lend()
    lend()

    for copy in early:
        copy.wait_recv()
    lhs[CHIP:CHIP + HALO] = edge[0, 16 - HALO:16]
    lhs[CHIP + HALO:CHIP + 2 * HALO] = edge[1, 0:HALO]
    local["lhs"].wait()
    rows.wait_recv()
    swapped = []

    def finish_coarse(path, coarse):
        axes, start, size = PATHS[path]
        columns = slice(start, start + size)
        part = 1.0 / (4.0 + shift[0] * coarse * coarse)
        invc[HALO:HALO + CHIP, columns] = part[:CHIP]
        invc[0:HALO, columns] = jnp.where(z > 0, part[CHIP:CHIP + HALO], 0.0)
        invc[HALO + CHIP:, columns] = jnp.where(z < SIDE - 1, part[CHIP + HALO:], 0.0)
        to = ds(core * HALF + start, size)
        swapped.append(links.start(invc.at[ds(other * ROWS, TALL), columns], inv.at[:, to], at(dc=1)))
        inv[:, to] = invc[ds(core * ROWS, TALL), columns]

    lefts, rights = {}, {}
    for k in range(SIDE):
        to = turn(x + (0, 3, 1, 2)[k], SIDE)
        lefts[0, k] = lefts[1, k] = lambda to=to: lhs[:, ds(to * 512, 512)]
        rights[0, k] = lambda to=to: fa[to].reshape(512, PATHS[0][2])
        rights[1, k] = lambda to=to: fb[to].reshape(512, PATHS[1][2])
        to = turn(y + (0, 3, 1, 2)[k], SIDE)
        lefts[2, k] = lambda to=to: jnp.concatenate([lhs[:, ds(m * 512 + to * BLOCK, BLOCK)] for m in range(SIDE)], axis=1)
        rights[2, k] = lambda to=to: fc[:, to].reshape(512, PATHS[2][2])

    for k in range(SIDE):
        for path, (axes, start, size) in enumerate(PATHS):
            if k == 3:
                if path == 0:
                    for step in range(SIDE):
                        for copy in passed[path, step]:
                            copy.wait_recv()
                else:
                    for copy in passed[path, k]:
                        copy.wait_recv()
            elif path:
                for copy in passed[path, k]:
                    copy.wait_recv()
            columns = slice(start, start + size)
            term = jnp.dot(lefts[path, k](), rights[path, k](), preferred_element_type=F32)
            if k == 0:
                partial[:, columns] = term
            elif k < 3:
                partial[:, columns] += term
            else:
                finish_coarse(path, partial[:, columns] + term)
    local["src"].wait()
    for copy in late + swapped:
        copy.wait_recv()
    for n in range(SIDE):
        columns = slice(n * 512, (n + 1) * 512)
        value = src[:, columns] * inv[:, columns]
        field[0, :, columns] = value
        narrow[0, :, columns] = value.astype(BF16)
    local["lat"].wait()
    local["rec"].wait()
    forwarded, crossed = [], []

    def pass_on(side, step, quarters):
        for quarter in range(SIDE):
            if quarter in quarters:
                lined[quarter][side].wait_recv()
                part = part_of(turn(z + 4 - step, SIDE) * 2 + core, quarter)
                forwarded.append(links.start(part, part, at(dz=step)))

    def cross(step):
        part = part_of(turn(z + step, SIDE) * 2 + core, 0, SIDE)
        crossed.append(links.start(part, part, at(dc=1)))

    pass_on(0, 1, (0, 1))
    for sweep in range(1, SWEEPS - 1):
        old, new = (sweep - 1) % 2, sweep % 2
        for n in range(SIDE):
            columns = slice(n * 512, (n + 1) * 512)
            side = jnp.dot(narrow[old], lat[:, columns], preferred_element_type=F32)
            before = field[old, :, columns]
            beside = pltpu.roll(before, 1, 0) + pltpu.roll(before, TALL - 1, 0)
            value = (src[:, columns] + 0.5 * beside + side) * inv[:, columns]
            field[new, :, columns] = value
            narrow[new, :, columns] = value.astype(BF16)
        if sweep == 1:
            pass_on(1, 3, (2, 3))
        if sweep == 2:
            for quarter in range(SIDE):
                if quarter < 2:
                    lined[quarter][1].wait_recv()
                else:
                    lined[quarter][0].wait_recv()
            cross(3)
            cross(1)
        if sweep == 5:
            for copy in forwarded:
                copy.wait_recv()
            cross(2)

    old = (SWEEPS - 2) % 2
    spans = {}
    for half in range(2):
        for pair in ((1, 2), (3, 4), (5, 6), (7, 0)):
            slices = [ds(turn(slab + d, SLABS) * WIDE + half * BLOCK, BLOCK) for d in pair]
            panel = jnp.concatenate([lat[:, columns] for columns in slices], axis=1)
            both = jnp.dot(narrow[old], panel, preferred_element_type=F32)
            for m, (d, columns) in enumerate(zip(pair, slices)):
                side = both[:, m * BLOCK:(m + 1) * BLOCK]
                before = field[old, :, columns]
                beside = pltpu.roll(before, 1, 0) + pltpu.roll(before, TALL - 1, 0)
                value = (src[:, columns] + 0.5 * beside + side) * inv[:, columns]
                part = (value[HALO:HALO + ROWS] * rec[:, columns]).T.astype(BF16)
                if d:
                    turned[half, d - 1] = part
                    spans[half, d] = links.start(turned.at[half, d - 1], gathered.at[half, :, here], line[d - 1])
                else:
                    gathered[half, :, here] = part

    beside_core.wait_recv()
    for copy in crossed:
        copy.wait_recv()
    first, second = {}, {}
    for half, me in ((0, x), (1, y)):
        for d in range(1, SLABS):
            spans[half, d].wait_recv()
        for d in (2, 1, 3, 0):
            to = turn(me + d, SIDE)
            if half == 0:
                panel = every[:, ds(to * 512, 512)]
            else:
                panel = jnp.concatenate([every[:, ds(m * 512 + to * BLOCK, BLOCK)] for m in range(SIDE)], axis=1)
            term = jnp.dot(gathered[half], panel, preferred_element_type=F32)
            if d:
                sent[half, d - 1] = term.astype(BF16)
                first[half, d] = links.start(sent.at[half, d - 1], came.at[half, d - 1], along(half, d))
            else:
                own[half] = term
    for half, it in ((0, y), (1, x)):
        total = own[half]
        for d in range(1, SIDE):
            first[half, d].wait_recv()
            total += came[half, d - 1].astype(F32)
        own[half] = total
        for m in range(SIDE):
            sums[half, m] = total[:, m * BLOCK:(m + 1) * BLOCK].astype(sums.dtype)
        for d in range(1, SIDE):
            second[half, d] = links.start(sums.at[half, turn(it + d, SIDE)], came2.at[half, d - 1], along(1 - half, d))
    for half, it in ((0, y), (1, x)):
        total = own[half, :, ds(it * BLOCK, BLOCK)]
        for d in range(1, SIDE):
            second[half, d].wait_recv()
            total += came2[half, d - 1].astype(F32)
        flat = total.T
        for s in range(SLABS):
            final[s, :, half * BLOCK:(half + 1) * BLOCK] = flat[s * 16:(s + 1) * 16]
    to = ds(slab * WIDE, WIDE)
    ends = []
    for d in range(1, SLABS):
        ends.append(links.start(final.at[turn(slab + d, SLABS)], image.at[:, to], line[d - 1]))
    image[:, to] = final[slab]
    for copy in ends:
        copy.wait_recv()
    links.finish()


COPIES = 160


def shards(fine_model, resample, lateral, shift, source, receiver):
    anywhere = pl.BlockSpec(memory_space=pl.ANY)
    vmem, dma = pltpu.VMEM, pltpu.SemaphoreType.DMA
    return pl.pallas_call(
        migrate,
        name="migrate",
        out_shape=jax.ShapeDtypeStruct((16, NL), F32),
        in_specs=[anywhere, anywhere, anywhere, pl.BlockSpec(memory_space=pltpu.SMEM), anywhere, anywhere],
        out_specs=pl.BlockSpec(memory_space=pltpu.VMEM),
        scratch_shapes=[
            *(vmem((SIDE, SIDE, SIDE, 32, size), BF16) for _, _, size in PATHS),
            vmem((CHIP + 2 * HALO, NL), BF16),
            vmem((2, 16, NL), BF16),
            vmem((SLABS * ROWS, NL), BF16),
            vmem((NL, NL), BF16),
            vmem((TALL, NL), F32),
            vmem((ROWS, NL), F32),
            vmem((CHIP + 2 * HALO, HALF), F32),
            vmem((CHIP + 2 * HALO, HALF), F32),
            vmem((TALL, NL), F32),
            vmem((2, TALL, NL), F32),
            vmem((2, TALL, NL), BF16),
            vmem((2, SLABS - 1, BLOCK, BLOCK), BF16),
            vmem((2, BLOCK, SLABS * BLOCK), BF16),
            vmem((2, BLOCK, 512), F32),
            vmem((2, 3, BLOCK, 512), BF16),
            vmem((2, 3, BLOCK, 512), BF16),
            vmem((2, SIDE, BLOCK, BLOCK), BF16),
            vmem((2, 3, BLOCK, BLOCK), BF16),
            vmem((SLABS, 16, WIDE), F32),
            dma((COPIES,)), dma((COPIES,)), dma((8,)),
        ],
        compiler_params=pltpu.CompilerParams(collective_id=0, has_side_effects=True, vmem_limit_bytes=56203264),
    )(fine_model, resample[0], lateral, shift, source[0], receiver[0])


def solution(mesh):
    in_specs = (
        P(("freq", "slab"), None),
        P("freq", "slab", None),
        P(),
        P("freq"),
        P("freq", "slab", None),
        P("freq", "slab", None),
    )
    out_specs = P(("freq", "slab"), None)
    return jax.shard_map(shards, mesh=mesh, in_specs=in_specs, out_specs=out_specs, check_vma=False)
```

time: 85.2 us -> 76.8 us (0.901)
  Pallas kernels: 82.8 us -> 74.5 us
    pallas_call x1, Pallas kernels: 82.8 us -> 74.5 us  [shards(): pl.pallas_call(migrate, name='migrate', out_shape=jax.ShapeDtypeStruct((1...]
where the time goes in v4:
time: 76.8 us; the launch traced here: 76.7 us
  Pallas kernels  74.5 us (97%)
  local copies, waits for them, and re-layouts  1.49 us (2%)
    pallas_call x1, Pallas kernels, shards(): pl.pallas_call(migrate, name='migrate', out_shape=jax.ShapeDtypeStruct((1...  74.5 us

profile of v4, /device:TPU:1, one launch (start us, length us, event | category | flops | bytes accessed | tf_op | source)
XLA Modules:
  0.0 76.7 jit_solution(3022309978609928129)
XLA Ops:
  0.7 0.0 copy-start
  0.7 0.8 %copy-done = bf16[16,2048]{1,0:T(8,128)(2,1)S(1)} copy-done((bf16[16,2048]{1,0:T(8,128)(2,1)S(1)}, bf16[16,2048]{1,0:T(8,128)(2,1)}, u32[]{:S(2)}) %copy-start) | copy-done | bytes 65560
  1.5 74.5 %migrate.1 = f32[16,2048]{1,0:T(8,128)S(1)} custom-call(bf16[16,2048]{1,0:T(8,128)(2,1)S(1)} %copy-done, bf16[128,2048]{1,0:T(8,128)(2,1)} %bitcast.5, bf16[2048,2048]{1,0:T(8,128)(2,1)} %lateral.1, f32[1]{0:T(128)S(6)} %copy.8.shift, f32[128,2048]{1,0:T(8,128)} %bitcast.3, f32[128,2048]{1,0:T(8,128)} %bitcast.4), custom_call_target="tpu_custom_call" | custom-call | tf_op jit(solution)/shard_map/migrate/pallas_call | solution.py:341
  76.0 0.7 copy.9
Async XLA Ops:
  0.7 0.8 %copy-start = (bf16[16,2048]{1,0:T(8,128)(2,1)S(1)}, bf16[16,2048]{1,0:T(8,128)(2,1)}, u32[]{:S(2)}) copy-start(bf16[16,2048]{1,0:T(8,128)(2,1)} %fine.1) | copy-start | bytes 196612

commit v5 on v4

--- a/solution.py
+++ b/solution.py
@@ -52,7 +52,7 @@
 
 def migrate(fine, oper, lateral, shift, source, receiver, image,
             fa, fb, fc, lhs, edge, every, lat, src, rec, partial, invc, inv, field, narrow,
-            turned, gathered, own, sent, came, sums, came2, final, send_sem, recv_sem, local_sem):
+            turned, gathered, own, sent, came, sums, landed, send_sem, recv_sem, local_sem):
     freq, slab = lax.axis_index("freq"), lax.axis_index("slab")
     x, y, z, core = freq // SIDE, turn(freq, SIDE), slab // 2, turn(slab, 2)
     other = 1 - core
@@ -288,7 +288,7 @@
     beside_core.wait_recv()
     for copy in crossed:
         copy.wait_recv()
-    first, second = {}, {}
+    first, second = {}, []
     for half, me in ((0, x), (1, y)):
         for d in range(1, SLABS):
             spans[half, d].wait_recv()
@@ -309,30 +309,25 @@
         for d in range(1, SIDE):
             first[half, d].wait_recv()
             total += came[half, d - 1].astype(F32)
-        own[half] = total
+        flat = total.T.astype(sums.dtype)
         for m in range(SIDE):
-            sums[half, m] = total[:, m * BLOCK:(m + 1) * BLOCK].astype(sums.dtype)
-        for d in range(1, SIDE):
-            second[half, d] = links.start(sums.at[half, turn(it + d, SIDE)], came2.at[half, d - 1], along(1 - half, d))
-    for half, it in ((0, y), (1, x)):
-        total = own[half, :, ds(it * BLOCK, BLOCK)]
-        for d in range(1, SIDE):
-            second[half, d].wait_recv()
-            total += came2[half, d - 1].astype(F32)
-        flat = total.T
-        for s in range(SLABS):
-            final[s, :, half * BLOCK:(half + 1) * BLOCK] = flat[s * 16:(s + 1) * 16]
-    to = ds(slab * WIDE, WIDE)
-    ends = []
-    for d in range(1, SLABS):
-        ends.append(links.start(final.at[turn(slab + d, SLABS)], image.at[:, to], line[d - 1]))
-    image[:, to] = final[slab]
-    for copy in ends:
+            for n in range(SLABS):
+                sums[half, m, n] = flat[m * BLOCK + n * 16:m * BLOCK + (n + 1) * 16]
+        to = ds(slab * WIDE + half * BLOCK, BLOCK)
+        for d in (2, 1, 3, 0):
+            for e in (4, 3, 5, 2, 6, 1, 7, 0):
+                if d or e:
+                    peer = along(1 - half, d)
+                    peer["slab"] = turn(slab + e, SLABS)
+                    second.append(links.start(sums.at[half, turn(it + d, SIDE), peer["slab"]], landed.at[d, :, to], peer))
+        landed[0, :, to] = sums[half, it, slab]
+    for copy in second:
         copy.wait_recv()
+    image[...] = ((landed[0].astype(F32) + landed[1].astype(F32)) + (landed[2].astype(F32) + landed[3].astype(F32)))
     links.finish()
 
 
-COPIES = 160
+COPIES = 210
 
 
 def shards(fine_model, resample, lateral, shift, source, receiver):
@@ -362,13 +357,12 @@
             vmem((2, BLOCK, 512), F32),
             vmem((2, 3, BLOCK, 512), BF16),
             vmem((2, 3, BLOCK, 512), BF16),
-            vmem((2, SIDE, BLOCK, BLOCK), BF16),
-            vmem((2, 3, BLOCK, BLOCK), BF16),
-            vmem((SLABS, 16, WIDE), F32),
+            vmem((2, SIDE, SLABS, 16, BLOCK), BF16),
+            vmem((SIDE, 16, NL), BF16),
             dma((COPIES,)), dma((COPIES,)), dma((8,)),
         ],
         compiler_params=pltpu.CompilerParams(collective_id=0, has_side_effects=True, vmem_limit_bytes=56203264),
-    )(fine_model, resample[0], lateral, shift, source[0], receiver[0])
+    )(pltpu.with_memory_space_constraint(fine_model, pltpu.HBM), resample[0], lateral, shift, source[0], receiver[0])
 
 
 def solution(mesh):

time: 76.8 us -> 74.2 us (0.966)
  Pallas kernels: 74.5 us -> 72.8 us
  local copies, waits for them, and re-layouts: 1.49 us -> 0.66 us
    pallas_call x1, Pallas kernels: 74.5 us -> 72.8 us  [shards(): pl.pallas_call(migrate, name='migrate', out_shape=jax.ShapeDtypeStruct((1...]
    unnamed x3 -> x1, local copies, waits for them, and re-layouts: 1.49 us -> 0.66 us
where the time goes in v5:
time: 74.2 us; the launch traced here: 74.1 us
  Pallas kernels  72.8 us (98%)
    pallas_call x1, Pallas kernels, shards(): pl.pallas_call(migrate, name='migrate', out_shape=jax.ShapeDtypeStruct((1...  72.8 us

profile of v5, /device:TPU:1, one launch (start us, length us, event | category | flops | bytes accessed | tf_op | source)
XLA Modules:
  0.0 74.1 jit_solution(7870325193764845662)
XLA Ops:
  0.7 72.8 %migrate.1 = f32[16,2048]{1,0:T(8,128)S(1)} custom-call(bf16[16,2048]{1,0:T(8,128)(2,1)} %fine.1, bf16[128,2048]{1,0:T(8,128)(2,1)} %bitcast.5, bf16[2048,2048]{1,0:T(8,128)(2,1)} %lateral.1, f32[1]{0:T(128)S(6)} %copy.8.shift, f32[128,2048]{1,0:T(8,128)} %bitcast.3, f32[128,2048]{1,0:T(8,128)} %bitcast.4), custom_call_target="tpu_custom_call" | custom-call | tf_op jit(solution)/shard_map/migrate/pallas_call | solution.py:336
  73.4 0.7 copy.9

commit v6 on v5

--- a/solution.py
+++ b/solution.py
@@ -240,7 +240,8 @@
         part = part_of(turn(z + step, SIDE) * 2 + core, 0, SIDE)
         crossed.append(links.start(part, part, at(dc=1)))
 
-    pass_on(0, 1, (0, 1))
+    pass_on(0, 1, (0,))
+    pass_on(1, 3, (1,))
     for sweep in range(1, SWEEPS - 1):
         old, new = (sweep - 1) % 2, sweep % 2
         for n in range(SIDE):
@@ -251,20 +252,14 @@
             value = (src[:, columns] + 0.5 * beside + side) * inv[:, columns]
             field[new, :, columns] = value
             narrow[new, :, columns] = value.astype(BF16)
-        if sweep == 1:
-            pass_on(1, 3, (2, 3))
-        if sweep == 2:
+        if sweep == 3:
+            pass_on(0, 1, (2,))
+            pass_on(1, 3, (3,))
+        if sweep == 4:
             for quarter in range(SIDE):
-                if quarter < 2:
-                    lined[quarter][1].wait_recv()
-                else:
-                    lined[quarter][0].wait_recv()
+                lined[quarter][1 - quarter % 2].wait_recv()
             cross(3)
             cross(1)
-        if sweep == 5:
-            for copy in forwarded:
-                copy.wait_recv()
-            cross(2)
 
     old = (SWEEPS - 2) % 2
     spans = {}
@@ -284,6 +279,10 @@
                     spans[half, d] = links.start(turned.at[half, d - 1], gathered.at[half, :, here], line[d - 1])
                 else:
                     gathered[half, :, here] = part
+        if half == 0:
+            for copy in forwarded:
+                copy.wait_recv()
+            cross(2)
 
     beside_core.wait_recv()
     for copy in crossed:

time: 74.2 us -> 72 us (0.970)
  Pallas kernels: 72.8 us -> 70.5 us
    pallas_call x1, Pallas kernels: 72.8 us -> 70.5 us  [shards(): pl.pallas_call(migrate, name='migrate', out_shape=jax.ShapeDtypeStruct((1...]
where the time goes in v6:
time: 72 us; the launch traced here: 71.9 us
  Pallas kernels  70.5 us (98%)
    pallas_call x1, Pallas kernels, shards(): pl.pallas_call(migrate, name='migrate', out_shape=jax.ShapeDtypeStruct((1...  70.5 us

profile of v6, /device:TPU:1, one launch (start us, length us, event | category | flops | bytes accessed | tf_op | source)
XLA Modules:
  0.0 71.9 jit_solution(2988799640325649744)
XLA Ops:
  0.7 70.5 %migrate.1 = f32[16,2048]{1,0:T(8,128)S(1)} custom-call(bf16[16,2048]{1,0:T(8,128)(2,1)} %fine.1, bf16[128,2048]{1,0:T(8,128)(2,1)} %bitcast.5, bf16[2048,2048]{1,0:T(8,128)(2,1)} %lateral.1, f32[1]{0:T(128)S(6)} %copy.8.shift, f32[128,2048]{1,0:T(8,128)} %bitcast.3, f32[128,2048]{1,0:T(8,128)} %bitcast.4), custom_call_target="tpu_custom_call" | custom-call | tf_op jit(solution)/shard_map/migrate/pallas_call | solution.py:335
  71.2 0.7 copy.9

commit v7 on v6

--- a/solution.py
+++ b/solution.py
@@ -218,15 +218,29 @@
             else:
                 finish_coarse(path, partial[:, columns] + term)
     local["src"].wait()
-    for copy in late + swapped:
-        copy.wait_recv()
+    for copy in late:
+        copy.wait_recv()
+
+    def begin(half):
+        for n in range(2):
+            columns = ds(half * HALF + n * 512, 512)
+            value = src[:, columns] * inv[:, columns]
+            field[0, :, columns] = value
+            narrow[0, :, columns] = value.astype(BF16)
+
+    def side_of(half, columns):
+        own_half = ds(half * HALF, HALF)
+        return jnp.dot(narrow[0, :, own_half], lat[own_half, columns], preferred_element_type=F32)
+
+    begin(core)
+    local["lat"].wait()
+    local["rec"].wait()
     for n in range(SIDE):
         columns = slice(n * 512, (n + 1) * 512)
-        value = src[:, columns] * inv[:, columns]
-        field[0, :, columns] = value
-        narrow[0, :, columns] = value.astype(BF16)
-    local["lat"].wait()
-    local["rec"].wait()
+        field[1, :, columns] = side_of(core, columns)
+    for copy in swapped:
+        copy.wait_recv()
+    begin(other)
     forwarded, crossed = [], []
 
     def pass_on(side, step, quarters):
@@ -246,7 +260,10 @@
         old, new = (sweep - 1) % 2, sweep % 2
         for n in range(SIDE):
             columns = slice(n * 512, (n + 1) * 512)
-            side = jnp.dot(narrow[old], lat[:, columns], preferred_element_type=F32)
+            if sweep == 1:
+                side = field[1, :, columns] + side_of(other, columns)
+            else:
+                side = jnp.dot(narrow[old], lat[:, columns], preferred_element_type=F32)
             before = field[old, :, columns]
             beside = pltpu.roll(before, 1, 0) + pltpu.roll(before, TALL - 1, 0)
             value = (src[:, columns] + 0.5 * beside + side) * inv[:, columns]
@@ -264,7 +281,7 @@
     old = (SWEEPS - 2) % 2
     spans = {}
     for half in range(2):
-        for pair in ((1, 2), (3, 4), (5, 6), (7, 0)):
+        for pair in ((4, 3), (5, 2), (6, 1), (7, 0)):
             slices = [ds(turn(slab + d, SLABS) * WIDE + half * BLOCK, BLOCK) for d in pair]
             panel = jnp.concatenate([lat[:, columns] for columns in slices], axis=1)
             both = jnp.dot(narrow[old], panel, preferred_element_type=F32)

time: 72 us -> 71.2 us (0.989)
  no operation moved by 1% of the time
where the time goes in v7:
time: 71.2 us; the launch traced here: 71.1 us
  Pallas kernels  69.8 us (98%)
    pallas_call x1, Pallas kernels, shards(): pl.pallas_call(migrate, name='migrate', out_shape=jax.ShapeDtypeStruct((1...  69.8 us

profile of v7, /device:TPU:1, one launch (start us, length us, event | category | flops | bytes accessed | tf_op | source)
XLA Modules:
  0.0 71.1 jit_solution(3228978318287569308)
XLA Ops:
  0.7 69.8 %migrate.1 = f32[16,2048]{1,0:T(8,128)S(1)} custom-call(bf16[16,2048]{1,0:T(8,128)(2,1)} %fine.1, bf16[128,2048]{1,0:T(8,128)(2,1)} %bitcast.5, bf16[2048,2048]{1,0:T(8,128)(2,1)} %lateral.1, f32[1]{0:T(128)S(6)} %copy.8.shift, f32[128,2048]{1,0:T(8,128)} %bitcast.3, f32[128,2048]{1,0:T(8,128)} %bitcast.4), custom_call_target="tpu_custom_call" | custom-call | tf_op jit(solution)/shard_map/migrate/pallas_call | solution.py:352
  70.5 0.7 copy.9
